TPU v7x, 32 devices: a whole 2x2x4 slice. The times are simulated.
32 devices in a mesh: fsdp: 32 (over z, y, x, core).
Axes of the slice: x: 2, y: 2, z: 4, core: 2. Of those that a mesh axis runs over, the one named last changes fastest.
Arguments:
- latents: bfloat16 [224, 256, 384], P('fsdp'), may hold values from -6 to 6
- cond: bfloat16 [224, 384], P('fsdp'), may hold values from -6 to 6
- live_counts: int32 [32], P('fsdp'), may hold values from 1 to 7, 149 in all
- ada_weight: bfloat16 [2, 384, 2304], P(None, None, 'fsdp'), may hold values from -0.3125 to 0.3125
- attn_weight: bfloat16 [2, 384, 1536], P(None, None, 'fsdp'), may hold values from -1 to 1
- mlp_in: bfloat16 [2, 384, 1536], P(None, None, 'fsdp'), may hold values from -0.3125 to 0.3125
- mlp_out: bfloat16 [2, 1536, 384], P(None, 'fsdp'), may hold values from -0.15625 to 0.15625
- bias_all: bfloat16 [2, 5376], P(None, 'fsdp'), may hold values from -3 to 3
- cotangent: bfloat16 [224, 256, 384], P('fsdp'), may hold values from -6 to 6
Outputs:
- activations: bfloat16 [224, 256, 384], P('fsdp')
- grad_latents: float32 [224, 256, 384], P('fsdp')
- grad_cond: float32 [224, 384], P('fsdp')
- grad_ada_weight: float32 [2, 384, 2304], P(None, None, 'fsdp')
- grad_attn_weight: float32 [2, 384, 1536], P(None, None, 'fsdp')
- grad_mlp_in: float32 [2, 384, 1536], P(None, None, 'fsdp')
- grad_mlp_out: float32 [2, 1536, 384], P(None, 'fsdp')
- grad_bias: float32 [2, 5376], P(None, 'fsdp')
Inputs may be any that keep to these rules, and one draw needn't show every extreme that they name: `live_counts`: the live latents of a device fill its first slots; the counts sum to 149.
All inputs are finite; a program needn't handle non-finite values.
Results may differ from a plain program's by a relative error of at most 0.013.
Values may be sent and summed in bfloat16 or wider, within the bound.
No kernel may reach another device: no remote copies, remote signals or barrier semaphores. Data moves between devices by JAX's collectives and lax.ppermute only.
A program may use at most 256 MiB of HBM per device.

v0:
```python
import jax
import jax.numpy as jnp
from jax import lax
from jax.experimental import pallas as pl
from jax.experimental.pallas import tpu as pltpu
from jax.sharding import PartitionSpec as P

HEADS = 6
D = 384
F = 1536
S = 256
BF = jnp.bfloat16
F32 = jnp.float32
SPLIT = 112
PAYLOAD = 224
BLOCKS = 32
ROWS = 144
AXIS = "fsdp"


def dot_nn(a, b):
    return lax.dot_general(a, b, (((1,), (0,)), ((), ())), preferred_element_type=F32)


def dot_nt(a, b):
    return lax.dot_general(a, b, (((1,), (1,)), ((), ())), preferred_element_type=F32)


def silu_value(v):
    return v / (1.0 + jnp.exp(-v))


def silu_slope(v):
    sigmoid = 1.0 / (1.0 + jnp.exp(-v))
    return sigmoid * (1.0 + v * (1.0 - sigmoid))


def layer_norm(v):
    centre = v - jnp.mean(v, -1, keepdims=True)
    spread = jnp.mean(centre * centre, -1, keepdims=True)
    inverse = lax.rsqrt(spread + 1e-06)
    return centre * inverse, inverse


def norm_back(e, y, inverse):
    first = jnp.mean(e, -1, keepdims=True)
    second = jnp.mean(e * y, -1, keepdims=True)
    return inverse * (e - first - y * second)


def gelu_parts(u):
    square = u * u
    tanh = jnp.tanh(u * (0.7978845608028654 + (0.7978845608028654 * 0.044715) * square))
    return square, tanh


def gelu_value(u):
    _, tanh = gelu_parts(u)
    half = 0.5 * u
    return half + half * tanh


def gelu_both(u):
    square, tanh = gelu_parts(u)
    half = 0.5 * u
    value = half + half * tanh
    inner = 0.7978845608028654 + (3 * 0.7978845608028654 * 0.044715) * square
    slope = 0.5 + 0.5 * tanh + half * (1.0 - tanh * tanh) * inner
    return value, slope


def stack_heads(pair):
    lane = lax.broadcasted_iota(jnp.int32, pair.shape, 1)
    zero = jnp.zeros_like(pair)
    return jnp.concatenate([jnp.where(lane < 64, pair, zero), jnp.where(lane >= 64, pair, zero)], axis=0)


def attn_weight_of(wv, low, high):
    return wv[low:high, 0:48, :].reshape((high - low) * 48, D)


def inner_chunk(wv, c, base):
    return wv[16 * c : 16 * c + 16, base : base + 48, :].reshape(768, D)


def tile_of(modulation, k):
    return modulation[:, k * D : (k + 1) * D]


def forward_body(r, mod, bias, wv, keep):
    qkv_ref, prob_ref, att_ref, br1_ref, mid_ref, inn_ref, br2_ref = keep
    normed, _ = layer_norm(r)
    hidden = (normed * (1.0 + tile_of(mod, 1)) + tile_of(mod, 0)).astype(BF)
    per = D // 48
    for part, at in ((0, 0), (1, None), (2, 1)):
        project = dot_nt(hidden, attn_weight_of(wv, part * per, part * per + per))
        if at is not None:
            project = project + tile_of(bias, at)
        qkv_ref[:, part * D : (part + 1) * D] = project.astype(BF)
    for pair in range(HEADS // 2):
        lo = pair * 128
        query = qkv_ref[:, lo : lo + 128] * jnp.asarray(0.125, BF)
        key = stack_heads(qkv_ref[:, D + lo : D + lo + 128])
        value = stack_heads(qkv_ref[:, 2 * D + lo : 2 * D + lo + 128])
        scores = dot_nt(query, key)
        for h in range(2):
            part = scores[:, h * S : (h + 1) * S]
            expo = jnp.exp(part - jnp.max(part, -1, keepdims=True))
            total = jnp.sum(expo, -1, keepdims=True)
            prob_ref[:, (2 * pair + h) * S : (2 * pair + h + 1) * S] = (expo * (1.0 / total)).astype(BF)
        probs = prob_ref[:, 2 * pair * S : (2 * pair + 2) * S]
        att_ref[:, lo : lo + 128] = dot_nn(probs, value).astype(BF)
    branch = dot_nt(att_ref[...], attn_weight_of(wv, 3 * per, 4 * per)) + tile_of(bias, 2)
    br1_ref[...] = branch
    middle = r + tile_of(mod, 2) * branch
    mid_ref[...] = middle
    normed, _ = layer_norm(middle)
    hidden = (normed * (1.0 + tile_of(mod, 4)) + tile_of(mod, 3)).astype(BF)
    branch = tile_of(bias, 3)
    for c in range(2):
        inner = dot_nt(hidden, inner_chunk(wv, c, 48)) + bias[:, 4 * D + 768 * c : 4 * D + 768 * (c + 1)]
        inn_ref[:, 768 * c : 768 * (c + 1)] = inner
        branch = branch + dot_nn(gelu_value(inner).astype(BF), inner_chunk(wv, c, 96))
    br2_ref[...] = branch
    return middle + tile_of(mod, 5) * branch


def column_sum(v):
    return jnp.sum(v, axis=0, keepdims=True)


def backward_body(g, r, mod, wv, keep, acc, dbias_ref, dmod_ref, row, dqkv_ref):
    qkv_ref, prob_ref, att_ref, br1_ref, mid_ref, inn_ref, br2_ref = keep
    acc_attn, acc_in, acc_out = acc
    per = D // 48

    def put(k, v):
        dmod_ref[pl.ds(row, 1), k * D : (k + 1) * D] = v

    def bias_add(lo, v):
        dbias_ref[:, lo : lo + v.shape[1]] += v

    d_br2 = (tile_of(mod, 5) * g).astype(BF)
    put(5, column_sum(g * br2_ref[...]))
    bias_add(3 * D, column_sum(d_br2.astype(F32)))
    d_br2_t = d_br2.T
    normed, inverse = layer_norm(mid_ref[...])
    scale = 1.0 + tile_of(mod, 4)
    hidden_t = (normed * scale + tile_of(mod, 3)).astype(BF).T
    d_hidden = None
    for c in range(2):
        cols = slice(768 * c, 768 * (c + 1))
        act, slope = gelu_both(inn_ref[:, cols])
        acc_out[:, cols] += dot_nn(d_br2_t, act.astype(BF))
        d_inner = (dot_nt(d_br2, inner_chunk(wv, c, 96)) * slope).astype(BF)
        bias_add(4 * D + 768 * c, column_sum(d_inner.astype(F32)))
        acc_in[:, cols] += dot_nn(hidden_t, d_inner)
        part = dot_nn(d_inner, inner_chunk(wv, c, 48))
        d_hidden = part if d_hidden is None else d_hidden + part
    put(4, column_sum(d_hidden * normed))
    put(3, column_sum(d_hidden))
    d_mid = g + norm_back(d_hidden * scale, normed, inverse)
    d_br1 = (tile_of(mod, 2) * d_mid).astype(BF)
    put(2, column_sum(d_mid * br1_ref[...]))
    bias_add(2 * D, column_sum(d_br1.astype(F32)))
    acc_attn[:, 3 * D : 4 * D] += dot_nn(att_ref[...].T, d_br1)
    d_att = dot_nn(d_br1, attn_weight_of(wv, 3 * per, 4 * per)).astype(BF)
    for pair in range(HEADS // 2):
        lo = pair * 128
        query = qkv_ref[:, lo : lo + 128] * jnp.asarray(0.125, BF)
        key = stack_heads(qkv_ref[:, D + lo : D + lo + 128])
        value = stack_heads(qkv_ref[:, 2 * D + lo : 2 * D + lo + 128])
        d_out = d_att[:, lo : lo + 128]
        both = d_out.astype(F32) * att_ref[:, lo : lo + 128].astype(F32)
        lane = lax.broadcasted_iota(jnp.int32, both.shape, 1)
        d_probs = dot_nt(d_out, value)
        pieces = []
        probs = []
        for h in range(2):
            chosen = lane < 64 if h == 0 else lane >= 64
            delta = jnp.sum(jnp.where(chosen, both, 0.0), -1, keepdims=True)
            prob = prob_ref[:, (2 * pair + h) * S : (2 * pair + h + 1) * S]
            probs.append(prob)
            pieces.append((prob.astype(F32) * (d_probs[:, h * S : (h + 1) * S] - delta)).astype(BF))
        d_query = (dot_nn(jnp.concatenate(pieces, axis=1), key) * 0.125).astype(BF)
        d_scores = jnp.concatenate(pieces, axis=0)
        d_key = dot_nn(split_rows(query.T), d_scores).T.astype(BF)
        d_value = dot_nn(split_rows(d_out.T), jnp.concatenate(probs, axis=0)).T.astype(BF)
        dqkv_ref[:, lo : lo + 128] = d_query
        dqkv_ref[:, D + lo : D + lo + 128] = d_key
        dqkv_ref[:, 2 * D + lo : 2 * D + lo + 128] = d_value
        bias_add(lo, column_sum(d_query.astype(F32)))
        bias_add(D + lo, column_sum(d_value.astype(F32)))
    normed, inverse = layer_norm(r)
    scale = 1.0 + tile_of(mod, 1)
    hidden_t = (normed * scale + tile_of(mod, 0)).astype(BF).T
    d_hidden = None
    for part in range(3):
        cols = slice(part * D, (part + 1) * D)
        d_part = dqkv_ref[:, cols]
        acc_attn[:, cols] += dot_nn(hidden_t, d_part)
        term = dot_nn(d_part, attn_weight_of(wv, part * per, part * per + per))
        d_hidden = term if d_hidden is None else d_hidden + term
    put(1, column_sum(d_hidden * normed))
    put(0, column_sum(d_hidden))
    return d_mid + norm_back(d_hidden * scale, normed, inverse)


def split_rows(pair):
    sub = lax.broadcasted_iota(jnp.int32, pair.shape, 0)
    zero = jnp.zeros_like(pair)
    return jnp.concatenate([jnp.where(sub < 64, pair, zero), jnp.where(sub >= 64, pair, zero)], axis=1)


def fetch_weights(table, pieces, wv, sem):
    copies = []
    for ref, (masks, low, rows) in pieces:
        for k, mask in enumerate(masks):
            block = table[mask]
            copies.append(
                pltpu.make_async_copy(
                    ref.at[k, pl.ds(0, rows), :], wv.at[block, pl.ds(low, rows), :], sem.at[len(copies)]
                )
            )
    for copy in copies:
        copy.start()
    for copy in copies:
        copy.wait()


def emit_grads(table, acc, stage, outs, orders, sem):
    for part, ref in enumerate(acc):
        for k in range(4):
            block = ref[:, k * D : (k + 1) * D].T.astype(BF)
            stage[8 * k : 8 * k + 8, 48 * part : 48 * part + 48, :] = block.reshape(8, 48, D)
    copies = []
    for ref, (masks, low, rows) in zip(outs, orders):
        for k, mask in enumerate(masks):
            copies.append(
                pltpu.make_async_copy(stage.at[table[mask], pl.ds(low, rows), :], ref.at[k], sem.at[len(copies)])
            )
    for copy in copies:
        copy.start()
    for copy in copies:
        copy.wait()


def saved_shapes():
    return [(3 * D, BF), (HEADS * S, BF), (D, BF), (D, F32), (D, F32), (F, F32), (D, F32)]


def run_forward(table, latents, mod, bias, pieces, layout):
    slots = latents.shape[0]
    count = len(pieces)

    def body(table_ref, lat_ref, mod_ref, bias_ref, *rest):
        piece_refs = rest[:count]
        keep = [ref.at[0] for ref in rest[count : count + 7]]
        out_ref, wv, sem = rest[count + 7 :]
        step = pl.program_id(0)

        @pl.when(step == 0)
        def _():
            fetch_weights(table_ref, list(zip(piece_refs, layout)), wv, sem)

        @pl.when(step < table_ref[BLOCKS])
        def _():
            out_ref[0] = forward_body(
                lat_ref[0].astype(F32), mod_ref[pl.ds(step, 1), :], bias_ref[...], wv, keep
            )

    clamp = lambda i, t: (jnp.minimum(i, t[BLOCKS] - 1), 0, 0)
    whole = lambda i, t: (0, 0)
    shapes = saved_shapes() + [(D, F32)]
    return pl.pallas_call(
        body,
        grid_spec=pltpu.PrefetchScalarGridSpec(
            num_scalar_prefetch=1,
            grid=(slots,),
            in_specs=[
                pl.BlockSpec((1, S, D), clamp),
                pl.BlockSpec(mod.shape, whole),
                pl.BlockSpec(bias.shape, whole),
            ]
            + [pl.BlockSpec(memory_space=pl.ANY)] * count,
            out_specs=[pl.BlockSpec((1, S, width), clamp) for width, _ in shapes],
            scratch_shapes=[
                pltpu.VMEM((32, ROWS, D), BF),
                pltpu.SemaphoreType.DMA((2 * BLOCKS,)),
            ],
        ),
        out_shape=[jax.ShapeDtypeStruct((slots, S, width), kind) for width, kind in shapes],
        cost_estimate=pl.CostEstimate(flops=slots * 1100000000, bytes_accessed=40000000, transcendentals=0),
        name="forward_zero",
    )(table, latents, mod, bias, *pieces)


def grad_outs():
    half = BLOCKS // 2
    shapes = [(half, SPLIT, D)] * 2 + [(half, ROWS - SPLIT, D)] * 2
    return [jax.ShapeDtypeStruct(shape, BF) for shape in shapes]


def run_middle(table, residual, cotangent, mod, bias, pieces, layout, orders):
    slots = residual.shape[0]
    count = len(pieces)

    def body(table_ref, res_ref, cot_ref, mod_ref, bias_ref, *rest):
        piece_refs = rest[:count]
        act_ref, g_ref, dmod_ref, dbias_ref = rest[count : count + 4]
        outs = rest[count + 4 : count + 8]
        wv, sem, a1, a2, a3, stage, dqkv = rest[count + 8 : count + 15]
        keep = rest[count + 15 :]
        acc = (a1, a2, a3)
        step = pl.program_id(0)

        @pl.when(step == 0)
        def _():
            fetch_weights(table_ref, list(zip(piece_refs, layout)), wv, sem)
            for ref in acc + (dbias_ref, dmod_ref):
                ref[...] = jnp.zeros_like(ref)

        @pl.when(step < table_ref[BLOCKS])
        def _():
            m = mod_ref[pl.ds(step, 1), :]
            r = res_ref[0]
            act_ref[0] = forward_body(r, m, bias_ref[...], wv, keep).astype(BF)
            g_ref[0] = backward_body(
                cot_ref[0].astype(F32), r, m, wv, keep, acc, dbias_ref, dmod_ref, step, dqkv
            )

        @pl.when(step >= table_ref[BLOCKS])
        def _():
            act_ref[0] = jnp.zeros((S, D), BF)

        @pl.when(step == slots - 1)
        def _():
            emit_grads(table_ref, acc, stage, outs, orders, sem)

    clamp = lambda i, t: (jnp.minimum(i, t[BLOCKS] - 1), 0, 0)
    each = lambda i, t: (i, 0, 0)
    whole = lambda i, t: (0, 0)
    any_spec = pl.BlockSpec(memory_space=pl.ANY)
    return pl.pallas_call(
        body,
        grid_spec=pltpu.PrefetchScalarGridSpec(
            num_scalar_prefetch=1,
            grid=(slots,),
            in_specs=[
                pl.BlockSpec((1, S, D), clamp),
                pl.BlockSpec((1, S, D), clamp),
                pl.BlockSpec(mod.shape, whole),
                pl.BlockSpec(bias.shape, whole),
            ]
            + [any_spec] * count,
            out_specs=[
                pl.BlockSpec((1, S, D), each),
                pl.BlockSpec((1, S, D), clamp),
                pl.BlockSpec((slots, 6 * D), whole),
                pl.BlockSpec((1, 8 * D), whole),
            ]
            + [any_spec] * 4,
            scratch_shapes=[
                pltpu.VMEM((32, ROWS, D), BF),
                pltpu.SemaphoreType.DMA((2 * BLOCKS,)),
                pltpu.VMEM((D, F), F32),
                pltpu.VMEM((D, F), F32),
                pltpu.VMEM((D, F), F32),
                pltpu.VMEM((32, ROWS, D), BF),
                pltpu.VMEM((S, 3 * D), BF),
            ]
            + [pltpu.VMEM((S, width), kind) for width, kind in saved_shapes()],
        ),
        out_shape=[
            jax.ShapeDtypeStruct((slots, S, D), BF),
            jax.ShapeDtypeStruct((slots, S, D), F32),
            jax.ShapeDtypeStruct((slots, 6 * D), F32),
            jax.ShapeDtypeStruct((1, 8 * D), F32),
        ]
        + grad_outs(),
        cost_estimate=pl.CostEstimate(flops=slots * 3300000000, bytes_accessed=20000000, transcendentals=0),
        name="middle_one",
    )(table, residual, cotangent, mod, bias, *pieces)


def run_backward(table, latents, upstream, mod, pieces, layout, saved, orders):
    slots = latents.shape[0]
    count = len(pieces)

    def body(table_ref, lat_ref, g_ref, mod_ref, *rest):
        keep = [ref.at[0] for ref in rest[:7]]
        piece_refs = rest[7 : 7 + count]
        rest = rest[7 + count :]
        out_ref, dmod_ref, dbias_ref = rest[:3]
        outs = rest[3:7]
        wv, sem, a1, a2, a3, stage, dqkv = rest[7:]
        acc = (a1, a2, a3)
        step = pl.program_id(0)

        @pl.when(step == 0)
        def _():
            fetch_weights(table_ref, list(zip(piece_refs, layout)), wv, sem)
            for ref in acc + (dbias_ref, dmod_ref):
                ref[...] = jnp.zeros_like(ref)

        @pl.when(step < table_ref[BLOCKS])
        def _():
            out_ref[0] = backward_body(
                g_ref[0],
                lat_ref[0].astype(F32),
                mod_ref[pl.ds(step, 1), :],
                wv,
                keep,
                acc,
                dbias_ref,
                dmod_ref,
                step,
                dqkv,
            )

        @pl.when(step >= table_ref[BLOCKS])
        def _():
            out_ref[0] = jnp.zeros((S, D), F32)

        @pl.when(step == slots - 1)
        def _():
            emit_grads(table_ref, acc, stage, outs, orders, sem)

    clamp = lambda i, t: (jnp.minimum(i, t[BLOCKS] - 1), 0, 0)
    each = lambda i, t: (i, 0, 0)
    whole = lambda i, t: (0, 0)
    any_spec = pl.BlockSpec(memory_space=pl.ANY)
    return pl.pallas_call(
        body,
        grid_spec=pltpu.PrefetchScalarGridSpec(
            num_scalar_prefetch=1,
            grid=(slots,),
            in_specs=[
                pl.BlockSpec((1, S, D), clamp),
                pl.BlockSpec((1, S, D), clamp),
                pl.BlockSpec(mod.shape, whole),
            ]
            + [pl.BlockSpec((1, S, width), clamp) for width, _ in saved_shapes()]
            + [any_spec] * count,
            out_specs=[
                pl.BlockSpec((1, S, D), each),
                pl.BlockSpec((slots, 6 * D), whole),
                pl.BlockSpec((1, 8 * D), whole),
            ]
            + [any_spec] * 4,
            scratch_shapes=[
                pltpu.VMEM((32, ROWS, D), BF),
                pltpu.SemaphoreType.DMA((2 * BLOCKS,)),
                pltpu.VMEM((D, F), F32),
                pltpu.VMEM((D, F), F32),
                pltpu.VMEM((D, F), F32),
                pltpu.VMEM((32, ROWS, D), BF),
                pltpu.VMEM((S, 3 * D), BF),
            ],
        ),
        out_shape=[
            jax.ShapeDtypeStruct((slots, S, D), F32),
            jax.ShapeDtypeStruct((slots, 6 * D), F32),
            jax.ShapeDtypeStruct((1, 8 * D), F32),
        ]
        + grad_outs(),
        cost_estimate=pl.CostEstimate(flops=slots * 2200000000, bytes_accessed=50000000, transcendentals=0),
        name="backward_zero",
    )(table, latents, upstream, mod, *saved, *pieces)


def permute(v, mask):
    size = lax.axis_size(AXIS)
    return lax.ppermute(v, AXIS, [(i, i ^ mask) for i in range(size)])


Z_MASKS = (0, 8, 16, 24)


def path_masks(first, second):
    order = [m for m in Z_MASKS]
    order = order + [m ^ second for m in order]
    return order + [m ^ first for m in order]


def tie(v, *after):
    return lax.optimization_barrier((v,) + after)[0]


def gather_line(shard):
    return jnp.stack([shard] + [permute(shard, m) for m in Z_MASKS[1:]])


def gather_near(line):
    one, two = line[:, :SPLIT], line[:, SPLIT:]
    near_one = jnp.concatenate([one, permute(one, 2)], axis=0)
    near_two = jnp.concatenate([two, permute(two, 4)], axis=0)
    return near_one, near_two


def gather_rest(near, far):
    return [near[0], far[0], permute(near[0], 1), permute(far[0], 1)], [
        near[1],
        far[1],
        permute(near[1], 1),
        permute(far[1], 1),
    ]


def gather_layout():
    layout = []
    for low, rows, masks in ((0, SPLIT, path_masks(4, 2)), (SPLIT, ROWS - SPLIT, path_masks(2, 4))):
        for core in (0, 1):
            for half in (0, 1):
                layout.append(([m ^ core for m in masks[8 * half : 8 * half + 8]], low, rows))
    return layout


def grad_orders():
    one, two = path_masks(4, 2), path_masks(2, 4)
    return [
        (one, 0, SPLIT),
        ([m ^ 1 for m in one], 0, SPLIT),
        (two, SPLIT, ROWS - SPLIT),
        ([m ^ 1 for m in two], SPLIT, ROWS - SPLIT),
    ]


def plain_layout():
    return [(list(range(BLOCKS)), 0, ROWS)]


def plain_orders():
    low, high = list(range(16)), list(range(16, 32))
    return [(low, 0, SPLIT), (high, 0, SPLIT), (low, SPLIT, ROWS - SPLIT), (high, SPLIT, ROWS - SPLIT)]


def added(*terms):
    total = terms[0].astype(F32)
    for term in terms[1:]:
        total = total + term.astype(F32)
    return total


def reduce_core(wide_grads, extra):
    keep1, send1, keep2, send2 = wide_grads
    keep2 = jnp.concatenate([keep2, extra[:16]], axis=1)
    send2 = jnp.concatenate([send2, extra[16:]], axis=1)
    return added(keep1, permute(send1, 1)).astype(BF), added(keep2, permute(send2, 1)).astype(BF)


def reduce_rest(one, two):
    one = added(one[:8], permute(one[8:], 4)).astype(BF)
    two = added(two[:8], permute(two[8:], 2)).astype(BF)
    one = added(one[:4], permute(one[4:], 2)).astype(BF)
    two = added(two[:4], permute(two[4:], 4)).astype(BF)
    both = jnp.concatenate([one, two], axis=1)
    return added(both[0], *[permute(both[k], Z_MASKS[k]) for k in range(1, 4)])


def rank_matrix(me):
    masks = path_masks(2, 4)
    masks = jnp.asarray(masks + [m ^ 1 for m in masks], jnp.int32)
    return (masks[None, :] ^ me) == jnp.arange(BLOCKS, dtype=jnp.int32)[:, None]


def per_device(
    latents, cond, live_counts, ada_weight, attn_weight, mlp_in, mlp_out, bias_all, cotangent
):
    slots = latents.shape[0]
    layers = ada_weight.shape[0]
    fast = lax.axis_size(AXIS) == BLOCKS
    size = lax.axis_size(AXIS)
    me = lax.axis_index(AXIS)
    order = jnp.arange(BLOCKS, dtype=jnp.int32)
    if fast:
        order = order ^ me
    table = jnp.concatenate([order, live_counts.astype(jnp.int32)])
    cond_value = cond.astype(F32)
    cond_low = silu_value(cond_value).astype(BF)
    ada_rows = ada_weight.shape[2]
    attn_rows = attn_weight.shape[2]
    bias_count = bias_all.shape[1]
    layout = gather_layout() if fast else plain_layout()
    orders = grad_orders() if fast else plain_orders()
    rank = rank_matrix(me) if fast else None

    def payload(layer):
        bias_row = jnp.pad(bias_all[layer], (0, D - bias_count))[None]
        if fast:
            bias_row = jnp.pad(bias_row, ((0, 7), (0, 0)))
        parts = [attn_weight[layer].T, mlp_in[layer].T, mlp_out[layer], ada_weight[layer].T, bias_row]
        return jnp.concatenate(parts, axis=0)

    def modulation(ada, bias):
        bias = bias.reshape(-1).astype(F32)
        modulate = jnp.einsum("sd,jed->sje", cond_low, ada, preferred_element_type=F32)
        if fast:
            modulate = jnp.einsum(
                "jp,spe->sje", rank.astype(F32), modulate, precision=lax.Precision.HIGHEST
            )
        return bias[None, 6 * D :], modulate.reshape(slots, 6 * D) + bias[: 6 * D]

    def unpack_fast(one, two):
        full = jnp.concatenate([p[:, ROWS - SPLIT :] for p in two], axis=0)
        ada = full[:, :ada_rows]
        bias = jnp.dot(rank.astype(BF), full[:, ada_rows, :bias_count], preferred_element_type=F32)
        return (one + two, ada) + modulation(ada, bias)

    def unpack_plain(full):
        parts = [full[:, k * attn_rows : (k + 1) * attn_rows].reshape(BLOCKS, 48, D) for k in range(3)]
        ada = full[:, 3 * attn_rows : 3 * attn_rows + ada_rows].reshape(BLOCKS, -1, D)
        bias = full[:, 3 * attn_rows + ada_rows, :bias_count]
        return ([jnp.concatenate(parts, axis=1)], ada) + modulation(ada, bias)

    def local_grads(layer, result, ada):
        grad_modulate, grad_bias = result[:2]
        grad_low = grad_modulate.astype(BF)
        bias_full = jnp.concatenate([jnp.sum(grad_low.astype(F32), axis=0), grad_bias[0]])
        grouped = grad_low.reshape(slots, BLOCKS, -1)
        bias_rows = bias_full.reshape(size, bias_count).astype(BF)
        if fast:
            grouped = jnp.einsum(
                "jp,sje->spe", rank.astype(BF), grouped, preferred_element_type=F32
            ).astype(BF)
            bias_rows = jnp.einsum("jp,je->pe", rank.astype(BF), bias_rows, preferred_element_type=F32)
        cond_part = jnp.einsum("sje,jed->sd", grouped, ada, preferred_element_type=F32)
        ada_grad = jnp.einsum("sje,sd->jed", grouped, cond_low, preferred_element_type=F32)
        tail = jnp.pad(bias_rows[:, None], ((0, 0), (0, 7 if fast else 0), (0, D - bias_count)))
        if fast:
            return cond_part, jnp.concatenate([ada_grad.astype(BF), tail.astype(BF)], axis=1)
        keep1, send1, keep2, send2 = result[2:]
        full = jnp.concatenate(
            [jnp.concatenate([keep1, send1], axis=0), jnp.concatenate([keep2, send2], axis=0)], axis=1
        )
        parts = [full[:, 48 * k : 48 * k + 48].reshape(size, attn_rows, D).astype(F32) for k in range(3)]
        parts = parts + [ada_grad.reshape(size, ada_rows, D), tail.astype(F32)]
        return cond_part, jnp.concatenate(parts, axis=1)

    cond_grad = jnp.zeros(cond_value.shape, F32)
    shards = [None] * layers
    if fast:
        line0 = gather_line(payload(0))
        line1 = gather_line(tie(payload(1), line0))
        near0 = gather_near(line0)
        far0 = (permute(near0[0], 4), permute(near0[1], 2))
        near1 = gather_near(tie(line1, *far0))
        block0 = unpack_fast(*gather_rest(near0, far0))
        far1 = (permute(near1[0], 4), permute(near1[1], 2))
        first_table = tie(table, *near1)
    else:
        full = [lax.all_gather(payload(layer), AXIS, axis=0, tiled=False) for layer in range(layers)]
        block0 = unpack_plain(full[0])
        first_table = table
    saved = run_forward(first_table, latents, block0[3], block0[2], block0[0], layout)
    if fast:
        block1 = unpack_fast(*gather_rest(near1, far1))
    else:
        block1 = unpack_plain(full[1])
    middle = run_middle(
        table, saved[7], cotangent, block1[3], block1[2], block1[0], layout, orders
    )
    output, upstream = middle[:2]
    cond_part, extra = local_grads(1, middle[2:], block1[1])
    cond_grad = cond_grad + cond_part
    last_table = table
    if fast:
        one1, two1 = reduce_core(middle[4:], extra)
        last_table = tie(table, one1, two1)
    else:
        shards[1] = lax.psum_scatter(extra, AXIS, scatter_dimension=0, tiled=False)
    last = run_backward(
        last_table, latents, upstream, block0[3], block0[0], layout, saved[:7], orders
    )
    grad_latents = last[0]
    cond_part, extra = local_grads(0, last[1:], block0[1])
    cond_grad = cond_grad + cond_part
    if fast:
        one0, two0 = reduce_core(last[3:], extra)
        shards[1] = reduce_rest(one1, two1)
        shards[0] = reduce_rest(one0, two0)
    else:
        shards[0] = lax.psum_scatter(extra, AXIS, scatter_dimension=0, tiled=False)
    cond_grad = cond_grad * silu_slope(cond_value)

    def stacked(pick):
        return jnp.stack([pick(shards[layer]) for layer in range(layers)])

    wide = 3 * attn_rows
    return (
        output,
        grad_latents,
        cond_grad,
        stacked(lambda s: s[wide : wide + ada_rows].T),
        stacked(lambda s: s[:attn_rows].T),
        stacked(lambda s: s[attn_rows : 2 * attn_rows].T),
        stacked(lambda s: s[2 * attn_rows : wide]),
        stacked(lambda s: s[wide + ada_rows, :bias_count]),
    )


def solution(mesh):
    token = P("fsdp", None, None)
    column = P(None, None, "fsdp")
    row = P(None, "fsdp", None)
    return jax.shard_map(
        per_device,
        mesh=mesh,
        in_specs=(token, P("fsdp", None), P("fsdp"), column, column, column, row, P(None, "fsdp"), token),
        out_specs=(token, token, P("fsdp", None), column, column, column, row, P(None, "fsdp")),
        check_vma=False,
    )
```

profile of v0, /device:TPU:0, one launch (start us, length us, event | category | flops | bytes accessed | tf_op | source)
XLA Modules:
  0.0 321.1 jit_solution(13647667823643227022)
XLA Ops:
  1.4 0.8 bitcast_dynamic-update-slice_fusion.3
  2.2 0.8 bitcast_dynamic-update-slice_fusion.2
  3.0 0.8 bitcast_dynamic-update-slice_fusion.6
  3.8 0.9 bitcast_dynamic-update-slice_fusion
  4.7 5.1 %collective-permute-start.2 = (bf16[224,384]{1,0:T(8,128)(2,1)S(1)}, bf16[224,384]{1,0:T(8,128)(2,1)S(1)}, u32[]{:S(2)}, u32[]{:S(2)}) collective-permute-start(bf16[224,384]{1,0:T(8,128)(2,1)S(1)} %constant_dynamic-update-slice_fusion.1), channel_id=1, source_target_pairs={{0,24},{1,25},{2,26},{3,27},{4,28},{5,29},{6,30},{7,31},{8,16},{9,... | collective-permute-start | bytes 516104 | tf_op jit(solution)/shard_map/ppermute | solution.py:474
  10.5 4.7 %collective-permute-done.2 = bf16[224,384]{1,0:T(8,128)(2,1)S(1)} collective-permute-done((bf16[224,384]{1,0:T(8,128)(2,1)S(1)}, bf16[224,384]{1,0:T(8,128)(2,1)S(1)}, u32[]{:S(2)}, u32[]{:S(2)}) %collective-permute-start.2) | collective-permute-done | bytes 172064 | tf_op jit(solution)/shard_map/ppermute | solution.py:474
  15.2 9.3 %collective-permute-done.1 = bf16[224,384]{1,0:T(8,128)(2,1)S(1)} collective-permute-done((bf16[224,384]{1,0:T(8,128)(2,1)S(1)}, bf16[224,384]{1,0:T(8,128)(2,1)S(1)}, u32[]{:S(2)}, u32[]{:S(2)}) %collective-permute-start.1) | collective-permute-done | bytes 172064 | tf_op jit(solution)/shard_map/ppermute | solution.py:474
  24.6 1.6 collective-permute-start.8
  26.2 1.5 collective-permute-start.6
  27.7 6.1 %collective-permute-done.8 = bf16[4,112,384]{2,1,0:T(8,128)(2,1)S(1)} collective-permute-done((bf16[4,112,384]{2,1,0:T(8,128)(2,1)S(1)}, bf16[4,112,384]{2,1,0:T(8,128)(2,1)S(1)}, u32[]{:S(2)}, u32[]{:S(2)}) %collective-permute-start.8) | collective-permute-done | bytes 344096 | tf_op jit(solution)/shard_map/ppermute | solution.py:474
  33.9 1.6 collective-permute-start.9
  35.5 0.9 pad_maximum_fusion.8.rest_0_.rest_7_
  36.4 1.5 collective-permute-start.7
  38.6 2.4 collective-permute-start.5
  41.0 2.1 collective-permute-start.3
  43.1 4.7 %collective-permute-done.5 = bf16[224,384]{1,0:T(8,128)(2,1)S(1)} collective-permute-done((bf16[224,384]{1,0:T(8,128)(2,1)S(1)}, bf16[224,384]{1,0:T(8,128)(2,1)S(1)}, u32[]{:S(2)}, u32[]{:S(2)}) %collective-permute-start.5) | collective-permute-done | bytes 172064 | tf_op jit(solution)/shard_map/ppermute | solution.py:474
  47.8 6.0 %collective-permute-done.4 = bf16[224,384]{1,0:T(8,128)(2,1)S(1)} collective-permute-done((bf16[224,384]{1,0:T(8,128)(2,1)S(1)}, bf16[224,384]{1,0:T(8,128)(2,1)S(1)}, u32[]{:S(2)}, u32[]{:S(2)}) %collective-permute-start.4) | collective-permute-done | bytes 172064 | tf_op jit(solution)/shard_map/ppermute | solution.py:474
  54.6 1.1 collective-permute-start.10
  56.5 1.1 slice.276
  58.5 3.9 %collective-permute-done.11 = bf16[4,112,384]{2,1,0:T(8,128)(2,1)S(1)} collective-permute-done((bf16[4,112,384]{2,1,0:T(8,128)(2,1)S(1)}, bf16[4,112,384]{2,1,0:T(8,128)(2,1)S(1)}, u32[]{:S(2)}, u32[]{:S(2)}) %collective-permute-start.11) | collective-permute-done | bytes 344096 | tf_op jit(solution)/shard_map/ppermute | solution.py:474
  62.5 2.5 collective-permute-done.10
  65.0 1.1 collective-permute-start.16
  66.1 0.9 pad_maximum_fusion.9.rest_0_
  68.7 0.9 fusion.10
  71.7 1.0 collective-permute-start.19
  72.7 9.4 %collective-permute-done.16.rest_5_ = bf16[8,112,384]{2,1,0:T(8,128)(2,1)} collective-permute-done((bf16[8,112,384]{2,1,0:T(8,128)(2,1)S(1)}, bf16[8,112,384]{2,1,0:T(8,128)(2,1)}, u32[]{:S(2)}, u32[]{:S(2)}) %collective-permute-start.16) | collective-permute-done | bytes 688160 | tf_op jit(solution)/shard_map/ppermute | solution.py:474
  82.1 18.1 %forward_zero.1 = (bf16[7,256,1152]{2,1,0:T(8,128)(2,1)}, bf16[7,256,1536]{2,1,0:T(8,128)(2,1)}, bf16[7,256,384]{2,1,0:T(8,128)(2,1)}, f32[7,256,384]{2,1,0:T(8,...) custom-call(s32[33]{0:T(128)} %pad_add_fusion.table_ref, ...), custom_call_target="tpu_custom_call" | custom-call | flops 7699999744 | bytes 40000000 | tf_op jit(solution)/shard_map/forward_zero/pallas_call | solution.py:275
  100.2 1.1 slice.284
  101.3 1.1 slice.285
  102.4 4.2 %collective-permute-start.21 = (bf16[8,112,384]{2,1,0:T(8,128)(2,1)}, bf16[8,112,384]{2,1,0:T(8,128)(2,1)S(1)}, u32[]{:S(2)}, u32[]{:S(2)}) collective-permute-start(bf16[8,112,384]{2,1,0:T(8,128)(2,1)} %collective-permute-done.19.rest_1_), channel_id=1, source_target_pairs={{0,1},{1,0},{2,3},{3,2},{4,5},{5,4},{6,7},{7,6},{8,9},{9,8},{10,11... | collective-permute-start | bytes 2064392 | tf_op jit(solution)/shard_map/ppermute | solution.py:474
  106.6 1.1 slice.286
  108.0 1.3 copy-done
  109.3 0.9 fusion.6
  112.3 0.9 copy-done.15
  113.2 33.1 %middle_one.1 = (bf16[7,256,384]{2,1,0:T(8,128)(2,1)}, f32[7,256,384]{2,1,0:T(8,128)}, f32[7,2304]{1,0:T(8,128)}, f32[1,3072]{1,0:T(1,128)}, bf16[16,112,384]{2,...) custom-call(s32[33]{0:T(128)} %pad_add_fusion.table_ref, ...), custom_call_target="tpu_custom_call" | custom-call | flops 23100000256 | bytes 20000000 | tf_op jit(solution)/shard_map/middle_one/pallas_call | solution.py:344
  147.0 0.9 fusion.89
  148.7 7.3 %collective-permute-start.22 = (bf16[16,112,384]{2,1,0:T(8,128)(2,1)}, bf16[16,112,384]{2,1,0:T(8,128)(2,1)S(1)}, u32[]{:S(2)}, u32[]{:S(2)}) collective-permute-start(bf16[16,112,384]{2,1,0:T(8,128)(2,1)} %get-tuple-element.41), channel_id=1, source_target_pairs={{0,1},{1,0},{2,3},{3,2},{4,5},{5,4},{6,7},{7,6},{8,9},{9,8},{10,11... | collective-permute-start | bytes 4128776 | tf_op jit(solution)/shard_map/ppermute | solution.py:474
  158.0 0.9 collective-permute-done.22
  159.3 1.0 slice.310
  160.3 0.9 collective-permute-done.23
  161.5 0.9 slice.314
  162.4 34.4 %collective-permute-start.33 = (bf16[8,112,384]{2,1,0:T(8,128)(2,1)}, bf16[8,112,384]{2,1,0:T(8,128)(2,1)}, u32[]{:S(2)}, u32[]{:S(2)}) collective-permute-start(bf16[8,112,384]{2,1,0:T(8,128)(2,1)} %slice.310), channel_id=1, source_target_pairs={{0,4},{1,5},{2,6},{3,7},{4,0},{5,1},{6,2},{7,3},{8,12},{9,13},{10,... | collective-permute-start | bytes 2064392 | tf_op jit(solution)/shard_map/ppermute | solution.py:474
  196.8 26.9 %backward_zero.1 = (f32[7,256,384]{2,1,0:T(8,128)}, f32[7,2304]{1,0:T(8,128)}, f32[1,3072]{1,0:T(1,128)}, bf16[16,112,384]{2,1,0:T(8,128)(2,1)}, bf16[16,112,384...) custom-call(s32[33]{0:T(128)} %pad_add_fusion.table_ref, bf16[7,256,384]{2,1,0:T(8,128)(2,1)} %lat_ref.3, ...), custom_call_target="tpu_custom_call" | custom-call | flops 15399999488 | bytes 50000000 | tf_op jit(solution)/shard_map/backward_zero/pallas_call | solution.py:433
  224.5 0.9 fusion.88
  226.1 1.0 collective-permute-start.35
  227.1 17.8 %collective-permute-start.24 = (bf16[16,112,384]{2,1,0:T(8,128)(2,1)}, bf16[16,112,384]{2,1,0:T(8,128)(2,1)S(1)}, u32[]{:S(2)}, u32[]{:S(2)}) collective-permute-start(bf16[16,112,384]{2,1,0:T(8,128)(2,1)} %get-tuple-element.58), channel_id=1, source_target_pairs={{0,1},{1,0},{2,3},{3,2},{4,5},{5,4},{6,7},{7,6},{8,9},{9,8},{10,11... | collective-permute-start | bytes 4128776 | tf_op jit(solution)/shard_map/ppermute | solution.py:474
  247.4 1.3 add_convert_fusion.5
  249.4 13.9 %collective-permute-start.36 = (bf16[4,112,384]{2,1,0:T(8,128)(2,1)S(1)}, bf16[4,112,384]{2,1,0:T(8,128)(2,1)S(1)}, u32[]{:S(2)}, u32[]{:S(2)}) collective-permute-start(bf16[4,112,384]{2,1,0:T(8,128)(2,1)S(1)} %slice.316), channel_id=1, source_target_pairs={{0,4},{1,5},{2,6},{3,7},{4,0},{5,1},{6,2},{7,3},{8,12},{9,13},{10,... | collective-permute-start | bytes 1032200 | tf_op jit(solution)/shard_map/ppermute | solution.py:474
  263.9 6.2 %collective-permute-done.36 = bf16[4,112,384]{2,1,0:T(8,128)(2,1)S(1)} collective-permute-done((bf16[4,112,384]{2,1,0:T(8,128)(2,1)S(1)}, bf16[4,112,384]{2,1,0:T(8,128)(2,1)S(1)}, u32[]{:S(2)}, u32[]{:S(2)}) %collective-permute-start.36) | collective-permute-done | bytes 344096 | tf_op jit(solution)/shard_map/ppermute | solution.py:474
  270.4 3.4 %collective-permute-start.38 = (bf16[224,384]{1,0:T(8,128)(2,1)S(1)}, bf16[224,384]{1,0:T(8,128)(2,1)S(1)}, u32[]{:S(2)}, u32[]{:S(2)}) collective-permute-start(bf16[224,384]{1,0:T(8,128)(2,1)S(1)} %get-tuple-element.77), channel_id=1, source_target_pairs={{0,16},{1,17},{2,18},{3,19},{4,20},{5,21},{6,22},{7,23},{8,24},{9,... | collective-permute-start | bytes 516104 | tf_op jit(solution)/shard_map/ppermute | solution.py:474
  274.3 1.8 collective-permute-start.25
  276.5 1.7 collective-permute-start.28
  278.3 1.2 fusion.25
  279.5 7.4 %collective-permute-done.38 = bf16[224,384]{1,0:T(8,128)(2,1)S(1)} collective-permute-done((bf16[224,384]{1,0:T(8,128)(2,1)S(1)}, bf16[224,384]{1,0:T(8,128)(2,1)S(1)}, u32[]{:S(2)}, u32[]{:S(2)}) %collective-permute-start.38) | collective-permute-done | bytes 172064 | tf_op jit(solution)/shard_map/ppermute | solution.py:474
  286.9 2.0 collective-permute-done.25
  289.1 3.9 %collective-permute-start.26 = (bf16[4,112,384]{2,1,0:T(8,128)(2,1)S(1)}, bf16[4,112,384]{2,1,0:T(8,128)(2,1)S(1)}, u32[]{:S(2)}, u32[]{:S(2)}) collective-permute-start(bf16[4,112,384]{2,1,0:T(8,128)(2,1)S(1)} %slice.295), channel_id=1, source_target_pairs={{0,2},{1,3},{2,0},{3,1},{4,6},{5,7},{6,4},{7,5},{8,10},{9,11},{10,... | collective-permute-start | bytes 1032200 | tf_op jit(solution)/shard_map/ppermute | solution.py:474
  293.5 1.5 collective-permute-start.29
  295.0 5.3 %collective-permute-done.26 = bf16[4,112,384]{2,1,0:T(8,128)(2,1)S(1)} collective-permute-done((bf16[4,112,384]{2,1,0:T(8,128)(2,1)S(1)}, bf16[4,112,384]{2,1,0:T(8,128)(2,1)S(1)}, u32[]{:S(2)}, u32[]{:S(2)}) %collective-permute-start.26) | collective-permute-done | bytes 344096 | tf_op jit(solution)/shard_map/ppermute | solution.py:474
  300.4 1.3 collective-permute-done.29
  301.9 1.6 collective-permute-start.30
  304.0 1.5 collective-permute-start.31
  305.5 6.3 %collective-permute-done.30 = bf16[224,384]{1,0:T(8,128)(2,1)S(1)} collective-permute-done((bf16[224,384]{1,0:T(8,128)(2,1)S(1)}, bf16[224,384]{1,0:T(8,128)(2,1)S(1)}, u32[]{:S(2)}, u32[]{:S(2)}) %collective-permute-start.30) | collective-permute-done | bytes 172064 | tf_op jit(solution)/shard_map/ppermute | solution.py:474
  311.8 1.1 collective-permute-done.32
  312.9 5.4 %collective-permute-done.31 = bf16[224,384]{1,0:T(8,128)(2,1)S(1)} collective-permute-done((bf16[224,384]{1,0:T(8,128)(2,1)S(1)}, bf16[224,384]{1,0:T(8,128)(2,1)S(1)}, u32[]{:S(2)}, u32[]{:S(2)}) %collective-permute-start.31) | collective-permute-done | bytes 172064 | tf_op jit(solution)/shard_map/ppermute | solution.py:474
  (163 shorter events, 25.6 us)
Async XLA Ops:
  4.7 10.5 %collective-permute-start.2 = (bf16[224,384]{1,0:T(8,128)(2,1)S(1)}, bf16[224,384]{1,0:T(8,128)(2,1)S(1)}, u32[]{:S(2)}, u32[]{:S(2)}) collective-permute-start(bf16[224,384]{1,0:T(8,128)(2,1)S(1)} %constant_dynamic-update-slice_fusion.1), channel_id=1, source_target_pairs={{0,24},{1,25},{2,26},{3,27},{4,28},{5,29},{6,30},{7,31},{8,16},{9,... | collective-permute-start | bytes 516104 | tf_op jit(solution)/shard_map/ppermute | solution.py:474
  9.9 14.6 %collective-permute-start.1 = (bf16[224,384]{1,0:T(8,128)(2,1)S(1)}, bf16[224,384]{1,0:T(8,128)(2,1)S(1)}, u32[]{:S(2)}, u32[]{:S(2)}) collective-permute-start(bf16[224,384]{1,0:T(8,128)(2,1)S(1)} %constant_dynamic-update-slice_fusion.1), channel_id=1, source_target_pairs={{0,16},{1,17},{2,18},{3,19},{4,20},{5,21},{6,22},{7,23},{8,24},{9,... | collective-permute-start | bytes 516104 | tf_op jit(solution)/shard_map/ppermute | solution.py:474
  9.9 14.6 %collective-permute-start = (bf16[224,384]{1,0:T(8,128)(2,1)S(1)}, bf16[224,384]{1,0:T(8,128)(2,1)S(1)}, u32[]{:S(2)}, u32[]{:S(2)}) collective-permute-start(bf16[224,384]{1,0:T(8,128)(2,1)S(1)} %constant_dynamic-update-slice_fusion.1), channel_id=1, source_target_pairs={{0,8},{1,9},{2,10},{3,11},{4,12},{5,13},{6,14},{7,15},{8,0},{9,1},... | collective-permute-start | bytes 516104 | tf_op jit(solution)/shard_map/ppermute | solution.py:474
  24.6 18.5 %copy-start.16 = (s32[32]{0:T(128)S(1)}, s32[32]{0:T(128)}, u32[]{:S(2)}) copy-start(s32[32]{0:T(128)} %constant.15.clone) | copy-start | bytes 388
  24.6 9.2 %collective-permute-start.8 = (bf16[4,112,384]{2,1,0:T(8,128)(2,1)S(1)}, bf16[4,112,384]{2,1,0:T(8,128)(2,1)S(1)}, u32[]{:S(2)}, u32[]{:S(2)}) collective-permute-start(bf16[4,112,384]{2,1,0:T(8,128)(2,1)S(1)} %get-tuple-element.80), channel_id=1, source_target_pairs={{0,4},{1,5},{2,6},{3,7},{4,0},{5,1},{6,2},{7,3},{8,12},{9,13},{10,... | collective-permute-start | bytes 1032200 | tf_op jit(solution)/shard_map/ppermute | solution.py:474
  26.2 9.3 %collective-permute-start.6 = (bf16[4,112,384]{2,1,0:T(8,128)(2,1)S(1)}, bf16[4,112,384]{2,1,0:T(8,128)(2,1)S(1)}, u32[]{:S(2)}, u32[]{:S(2)}) collective-permute-start(bf16[4,112,384]{2,1,0:T(8,128)(2,1)S(1)} %get-tuple-element.81), channel_id=1, source_target_pairs={{0,2},{1,3},{2,0},{3,1},{4,6},{5,7},{6,4},{7,5},{8,10},{9,11},{10,... | collective-permute-start | bytes 1032200 | tf_op jit(solution)/shard_map/ppermute | solution.py:474
  33.9 20.0 %copy-start.6 = (bf16[8,112,384]{2,1,0:T(8,128)(2,1)}, bf16[8,112,384]{2,1,0:T(8,128)(2,1)S(1)}, u32[]{:S(2)}) copy-start(bf16[8,112,384]{2,1,0:T(8,128)(2,1)S(1)} %pad_maximum_fusion.4.rest_4_.rest_11_) | copy-start | bytes 2064388
  33.9 19.9 %collective-permute-start.9 = (bf16[8,112,384]{2,1,0:T(8,128)(2,1)S(1)}, bf16[8,112,384]{2,1,0:T(8,128)(2,1)}, u32[]{:S(2)}, u32[]{:S(2)}) collective-permute-start(bf16[8,112,384]{2,1,0:T(8,128)(2,1)S(1)} %pad_maximum_fusion.4.rest_4_.rest_11_), channel_id=1, source_target_pairs={{0,2},{1,3},{2,0},{3,1},{4,6},{5,7},{6,4},{7,5},{8,10},{9,11},{10,... | collective-permute-start | bytes 2064392 | tf_op jit(solution)/shard_map/ppermute | solution.py:474
  36.4 17.4 %collective-permute-start.7 = (bf16[8,112,384]{2,1,0:T(8,128)(2,1)}, bf16[8,112,384]{2,1,0:T(8,128)(2,1)}, u32[]{:S(2)}, u32[]{:S(2)}) collective-permute-start(bf16[8,112,384]{2,1,0:T(8,128)(2,1)} %pad_maximum_fusion.8.rest_0_.rest_7_), channel_id=1, source_target_pairs={{0,4},{1,5},{2,6},{3,7},{4,0},{5,1},{6,2},{7,3},{8,12},{9,13},{10,... | collective-permute-start | bytes 2064392 | tf_op jit(solution)/shard_map/ppermute | solution.py:474
  38.6 9.1 %collective-permute-start.5 = (bf16[224,384]{1,0:T(8,128)(2,1)S(1)}, bf16[224,384]{1,0:T(8,128)(2,1)S(1)}, u32[]{:S(2)}, u32[]{:S(2)}) collective-permute-start(bf16[224,384]{1,0:T(8,128)(2,1)S(1)} %constant_dynamic-update-slice_fusion), channel_id=1, source_target_pairs={{0,24},{1,25},{2,26},{3,27},{4,28},{5,29},{6,30},{7,31},{8,16},{9,... | collective-permute-start | bytes 516104 | tf_op jit(solution)/shard_map/ppermute | solution.py:474
  41.0 12.8 %collective-permute-start.4 = (bf16[224,384]{1,0:T(8,128)(2,1)S(1)}, bf16[224,384]{1,0:T(8,128)(2,1)S(1)}, u32[]{:S(2)}, u32[]{:S(2)}) collective-permute-start(bf16[224,384]{1,0:T(8,128)(2,1)S(1)} %constant_dynamic-update-slice_fusion), channel_id=1, source_target_pairs={{0,16},{1,17},{2,18},{3,19},{4,20},{5,21},{6,22},{7,23},{8,24},{9,... | collective-permute-start | bytes 516104 | tf_op jit(solution)/shard_map/ppermute | solution.py:474
  41.0 12.8 %collective-permute-start.3 = (bf16[224,384]{1,0:T(8,128)(2,1)S(1)}, bf16[224,384]{1,0:T(8,128)(2,1)S(1)}, u32[]{:S(2)}, u32[]{:S(2)}) collective-permute-start(bf16[224,384]{1,0:T(8,128)(2,1)S(1)} %constant_dynamic-update-slice_fusion), channel_id=1, source_target_pairs={{0,8},{1,9},{2,10},{3,11},{4,12},{5,13},{6,14},{7,15},{8,0},{9,1},... | collective-permute-start | bytes 516104 | tf_op jit(solution)/shard_map/ppermute | solution.py:474
  47.8 9.8 %collective-permute-start.12 = (bf16[8,112,384]{2,1,0:T(8,128)(2,1)S(1)}, bf16[8,112,384]{2,1,0:T(8,128)(2,1)S(1)}, u32[]{:S(2)}, u32[]{:S(2)}) collective-permute-start(bf16[8,112,384]{2,1,0:T(8,128)(2,1)S(1)} %pad_maximum_fusion.4.rest_4_.rest_11_), channel_id=1, source_target_pairs={{0,1},{1,0},{2,3},{3,2},{4,5},{5,4},{6,7},{7,6},{8,9},{9,8},{10,11... | collective-permute-start | bytes 2064392 | tf_op jit(solution)/shard_map/ppermute | solution.py:474
  54.0 8.4 %collective-permute-start.11 = (bf16[4,112,384]{2,1,0:T(8,128)(2,1)S(1)}, bf16[4,112,384]{2,1,0:T(8,128)(2,1)S(1)}, u32[]{:S(2)}, u32[]{:S(2)}) collective-permute-start(bf16[4,112,384]{2,1,0:T(8,128)(2,1)S(1)} %get-tuple-element.78), channel_id=1, source_target_pairs={{0,4},{1,5},{2,6},{3,7},{4,0},{5,1},{6,2},{7,3},{8,12},{9,13},{10,... | collective-permute-start | bytes 1032200 | tf_op jit(solution)/shard_map/ppermute | solution.py:474
  54.5 12.5 %collective-permute-start.13 = (bf16[8,112,384]{2,1,0:T(8,128)(2,1)}, bf16[8,112,384]{2,1,0:T(8,128)(2,1)S(1)}, u32[]{:S(2)}, u32[]{:S(2)}) collective-permute-start(bf16[8,112,384]{2,1,0:T(8,128)(2,1)} %collective-permute-done.9.rest_5_.rest_12_), channel_id=1, source_target_pairs={{0,1},{1,0},{2,3},{3,2},{4,5},{5,4},{6,7},{7,6},{8,9},{9,8},{10,11... | collective-permute-start | bytes 2064392 | tf_op jit(solution)/shard_map/ppermute | solution.py:474
  54.6 10.5 %collective-permute-start.10 = (bf16[4,112,384]{2,1,0:T(8,128)(2,1)S(1)}, bf16[4,112,384]{2,1,0:T(8,128)(2,1)S(1)}, u32[]{:S(2)}, u32[]{:S(2)}) collective-permute-start(bf16[4,112,384]{2,1,0:T(8,128)(2,1)S(1)} %get-tuple-element.79), channel_id=1, source_target_pairs={{0,2},{1,3},{2,0},{3,1},{4,6},{5,7},{6,4},{7,5},{8,10},{9,11},{10,... | collective-permute-start | bytes 1032200 | tf_op jit(solution)/shard_map/ppermute | solution.py:474
  56.2 15.5 %collective-permute-start.14 = (bf16[8,112,384]{2,1,0:T(8,128)(2,1)}, bf16[8,112,384]{2,1,0:T(8,128)(2,1)}, u32[]{:S(2)}, u32[]{:S(2)}) collective-permute-start(bf16[8,112,384]{2,1,0:T(8,128)(2,1)} %pad_maximum_fusion.8.rest_0_.rest_7_), channel_id=1, source_target_pairs={{0,1},{1,0},{2,3},{3,2},{4,5},{5,4},{6,7},{7,6},{8,9},{9,8},{10,11... | collective-permute-start | bytes 2064392 | tf_op jit(solution)/shard_map/ppermute | solution.py:474
  57.6 0.9 copy-start.12
  57.6 24.5 %collective-permute-start.15 = (bf16[8,112,384]{2,1,0:T(8,128)(2,1)}, bf16[8,112,384]{2,1,0:T(8,128)(2,1)}, u32[]{:S(2)}, u32[]{:S(2)}) collective-permute-start(bf16[8,112,384]{2,1,0:T(8,128)(2,1)} %collective-permute-done.7.rest_1_.rest_8_), channel_id=1, source_target_pairs={{0,1},{1,0},{2,3},{3,2},{4,5},{5,4},{6,7},{7,6},{8,9},{9,8},{10,11... | collective-permute-start | bytes 2064392 | tf_op jit(solution)/shard_map/ppermute | solution.py:474
  62.4 5.6 %copy-start.7 = (bf16[8,112,384]{2,1,0:T(8,128)(2,1)}, bf16[8,112,384]{2,1,0:T(8,128)(2,1)S(1)}, u32[]{:S(2)}) copy-start(bf16[8,112,384]{2,1,0:T(8,128)(2,1)S(1)} %pad_maximum_fusion.5.rest_4_) | copy-start | bytes 2064388
  62.4 38.9 %collective-permute-start.17 = (bf16[8,112,384]{2,1,0:T(8,128)(2,1)S(1)}, bf16[8,112,384]{2,1,0:T(8,128)(2,1)}, u32[]{:S(2)}, u32[]{:S(2)}) collective-permute-start(bf16[8,112,384]{2,1,0:T(8,128)(2,1)S(1)} %pad_maximum_fusion.5.rest_4_), channel_id=1, source_target_pairs={{0,1},{1,0},{2,3},{3,2},{4,5},{5,4},{6,7},{7,6},{8,9},{9,8},{10,11... | collective-permute-start | bytes 2064392 | tf_op jit(solution)/shard_map/ppermute | solution.py:474
  65.0 17.1 %collective-permute-start.16 = (bf16[8,112,384]{2,1,0:T(8,128)(2,1)S(1)}, bf16[8,112,384]{2,1,0:T(8,128)(2,1)}, u32[]{:S(2)}, u32[]{:S(2)}) collective-permute-start(bf16[8,112,384]{2,1,0:T(8,128)(2,1)S(1)} %pad_maximum_fusion.5.rest_4_), channel_id=1, source_target_pairs={{0,2},{1,3},{2,0},{3,1},{4,6},{5,7},{6,4},{7,5},{8,10},{9,11},{10,... | collective-permute-start | bytes 2064392 | tf_op jit(solution)/shard_map/ppermute | solution.py:474
  67.1 0.8 copy-start.13
  67.1 45.2 %collective-permute-start.20 = (bf16[8,112,384]{2,1,0:T(8,128)(2,1)}, bf16[8,112,384]{2,1,0:T(8,128)(2,1)}, u32[]{:S(2)}, u32[]{:S(2)}) collective-permute-start(bf16[8,112,384]{2,1,0:T(8,128)(2,1)} %pad_maximum_fusion.9.rest_0_), channel_id=1, source_target_pairs={{0,1},{1,0},{2,3},{3,2},{4,5},{5,4},{6,7},{7,6},{8,9},{9,8},{10,11... | collective-permute-start | bytes 2064392 | tf_op jit(solution)/shard_map/ppermute | solution.py:474
  68.0 0.7 copy-start.14
  71.7 30.7 %collective-permute-start.19 = (bf16[8,112,384]{2,1,0:T(8,128)(2,1)}, bf16[8,112,384]{2,1,0:T(8,128)(2,1)}, u32[]{:S(2)}, u32[]{:S(2)}) collective-permute-start(bf16[8,112,384]{2,1,0:T(8,128)(2,1)} %pad_maximum_fusion.9.rest_0_), channel_id=1, source_target_pairs={{0,4},{1,5},{2,6},{3,7},{4,0},{5,1},{6,2},{7,3},{8,12},{9,13},{10,... | collective-permute-start | bytes 2064392 | tf_op jit(solution)/shard_map/ppermute | solution.py:474
  82.1 24.5 %collective-permute-start.18 = (bf16[8,112,384]{2,1,0:T(8,128)(2,1)}, bf16[8,112,384]{2,1,0:T(8,128)(2,1)}, u32[]{:S(2)}, u32[]{:S(2)}) collective-permute-start(bf16[8,112,384]{2,1,0:T(8,128)(2,1)} %collective-permute-done.16.rest_5_), channel_id=1, source_target_pairs={{0,1},{1,0},{2,3},{3,2},{4,5},{5,4},{6,7},{7,6},{8,9},{9,8},{10,11... | collective-permute-start | bytes 2064392 | tf_op jit(solution)/shard_map/ppermute | solution.py:474
  102.4 9.9 %collective-permute-start.21 = (bf16[8,112,384]{2,1,0:T(8,128)(2,1)}, bf16[8,112,384]{2,1,0:T(8,128)(2,1)S(1)}, u32[]{:S(2)}, u32[]{:S(2)}) collective-permute-start(bf16[8,112,384]{2,1,0:T(8,128)(2,1)} %collective-permute-done.19.rest_1_), channel_id=1, source_target_pairs={{0,1},{1,0},{2,3},{3,2},{4,5},{5,4},{6,7},{7,6},{8,9},{9,8},{10,11... | collective-permute-start | bytes 2064392 | tf_op jit(solution)/shard_map/ppermute | solution.py:474
  108.0 1.3 copy-start
  112.3 0.9 copy-start.15
  148.7 10.2 %collective-permute-start.22 = (bf16[16,112,384]{2,1,0:T(8,128)(2,1)}, bf16[16,112,384]{2,1,0:T(8,128)(2,1)S(1)}, u32[]{:S(2)}, u32[]{:S(2)}) collective-permute-start(bf16[16,112,384]{2,1,0:T(8,128)(2,1)} %get-tuple-element.41), channel_id=1, source_target_pairs={{0,1},{1,0},{2,3},{3,2},{4,5},{5,4},{6,7},{7,6},{8,9},{9,8},{10,11... | collective-permute-start | bytes 4128776 | tf_op jit(solution)/shard_map/ppermute | solution.py:474
  156.8 1.0 copy-start.9
  157.0 1.9 copy-start.5
  158.0 3.2 collective-permute-start.23
  158.9 2.3 copy-start.11
  159.3 1.9 copy-start.2
  162.4 84.6 %collective-permute-start.33 = (bf16[8,112,384]{2,1,0:T(8,128)(2,1)}, bf16[8,112,384]{2,1,0:T(8,128)(2,1)}, u32[]{:S(2)}, u32[]{:S(2)}) collective-permute-start(bf16[8,112,384]{2,1,0:T(8,128)(2,1)} %slice.310), channel_id=1, source_target_pairs={{0,4},{1,5},{2,6},{3,7},{4,0},{5,1},{6,2},{7,3},{8,12},{9,13},{10,... | collective-permute-start | bytes 2064392 | tf_op jit(solution)/shard_map/ppermute | solution.py:474
  226.1 23.0 %collective-permute-start.35 = (bf16[8,112,384]{2,1,0:T(8,128)(2,1)}, bf16[8,112,384]{2,1,0:T(8,128)(2,1)S(1)}, u32[]{:S(2)}, u32[]{:S(2)}) collective-permute-start(bf16[8,112,384]{2,1,0:T(8,128)(2,1)} %slice.314), channel_id=1, source_target_pairs={{0,2},{1,3},{2,0},{3,1},{4,6},{5,7},{6,4},{7,5},{8,10},{9,11},{10,... | collective-permute-start | bytes 2064392 | tf_op jit(solution)/shard_map/ppermute | solution.py:474
  227.1 46.7 %collective-permute-start.24 = (bf16[16,112,384]{2,1,0:T(8,128)(2,1)}, bf16[16,112,384]{2,1,0:T(8,128)(2,1)S(1)}, u32[]{:S(2)}, u32[]{:S(2)}) collective-permute-start(bf16[16,112,384]{2,1,0:T(8,128)(2,1)} %get-tuple-element.58), channel_id=1, source_target_pairs={{0,1},{1,0},{2,3},{3,2},{4,5},{5,4},{6,7},{7,6},{8,9},{9,8},{10,11... | collective-permute-start | bytes 4128776 | tf_op jit(solution)/shard_map/ppermute | solution.py:474
  245.8 1.0 copy-start.8
  246.0 1.4 copy-start.3
  246.9 29.2 %collective-permute-start.27 = (bf16[16,112,384]{2,1,0:T(8,128)(2,1)S(1)}, bf16[16,112,384]{2,1,0:T(8,128)(2,1)S(1)}, u32[]{:S(2)}, u32[]{:S(2)}) collective-permute-start(bf16[16,112,384]{2,1,0:T(8,128)(2,1)S(1)} %pad_maximum_fusion.3), channel_id=1, source_target_pairs={{0,1},{1,0},{2,3},{3,2},{4,5},{5,4},{6,7},{7,6},{8,9},{9,8},{10,11... | collective-permute-start | bytes 4128776 | tf_op jit(solution)/shard_map/ppermute | solution.py:474
  248.7 15.1 %collective-permute-start.34 = (bf16[4,112,384]{2,1,0:T(8,128)(2,1)S(1)}, bf16[4,112,384]{2,1,0:T(8,128)(2,1)S(1)}, u32[]{:S(2)}, u32[]{:S(2)}) collective-permute-start(bf16[4,112,384]{2,1,0:T(8,128)(2,1)S(1)} %slice.312), channel_id=1, source_target_pairs={{0,2},{1,3},{2,0},{3,1},{4,6},{5,7},{6,4},{7,5},{8,10},{9,11},{10,... | collective-permute-start | bytes 1032200 | tf_op jit(solution)/shard_map/ppermute | solution.py:474
  249.4 20.7 %collective-permute-start.36 = (bf16[4,112,384]{2,1,0:T(8,128)(2,1)S(1)}, bf16[4,112,384]{2,1,0:T(8,128)(2,1)S(1)}, u32[]{:S(2)}, u32[]{:S(2)}) collective-permute-start(bf16[4,112,384]{2,1,0:T(8,128)(2,1)S(1)} %slice.316), channel_id=1, source_target_pairs={{0,4},{1,5},{2,6},{3,7},{4,0},{5,1},{6,2},{7,3},{8,12},{9,13},{10,... | collective-permute-start | bytes 1032200 | tf_op jit(solution)/shard_map/ppermute | solution.py:474
  263.8 10.0 %copy-start.4 = (bf16[16,112,384]{2,1,0:T(8,128)(2,1)S(1)}, bf16[16,112,384]{2,1,0:T(8,128)(2,1)}, u32[]{:S(2)}) copy-start(bf16[16,112,384]{2,1,0:T(8,128)(2,1)} %get-tuple-element.57) | copy-start | bytes 4128772
  270.2 9.2 %collective-permute-start.37 = (bf16[224,384]{1,0:T(8,128)(2,1)S(1)}, bf16[224,384]{1,0:T(8,128)(2,1)S(1)}, u32[]{:S(2)}, u32[]{:S(2)}) collective-permute-start(bf16[224,384]{1,0:T(8,128)(2,1)S(1)} %get-tuple-element.75), channel_id=1, source_target_pairs={{0,8},{1,9},{2,10},{3,11},{4,12},{5,13},{6,14},{7,15},{8,0},{9,1},... | collective-permute-start | bytes 516104 | tf_op jit(solution)/shard_map/ppermute | solution.py:474
  270.3 9.2 %collective-permute-start.39 = (bf16[224,384]{1,0:T(8,128)(2,1)S(1)}, bf16[224,384]{1,0:T(8,128)(2,1)S(1)}, u32[]{:S(2)}, u32[]{:S(2)}) collective-permute-start(bf16[224,384]{1,0:T(8,128)(2,1)S(1)} %get-tuple-element.76), channel_id=1, source_target_pairs={{0,24},{1,25},{2,26},{3,27},{4,28},{5,29},{6,30},{7,31},{8,16},{9,... | collective-permute-start | bytes 516104 | tf_op jit(solution)/shard_map/ppermute | solution.py:474
  270.4 16.5 %collective-permute-start.38 = (bf16[224,384]{1,0:T(8,128)(2,1)S(1)}, bf16[224,384]{1,0:T(8,128)(2,1)S(1)}, u32[]{:S(2)}, u32[]{:S(2)}) collective-permute-start(bf16[224,384]{1,0:T(8,128)(2,1)S(1)} %get-tuple-element.77), channel_id=1, source_target_pairs={{0,16},{1,17},{2,18},{3,19},{4,20},{5,21},{6,22},{7,23},{8,24},{9,... | collective-permute-start | bytes 516104 | tf_op jit(solution)/shard_map/ppermute | solution.py:474
  273.8 2.3 copy-start.10
  274.3 14.6 %collective-permute-start.25 = (bf16[8,112,384]{2,1,0:T(8,128)(2,1)S(1)}, bf16[8,112,384]{2,1,0:T(8,128)(2,1)S(1)}, u32[]{:S(2)}, u32[]{:S(2)}) collective-permute-start(bf16[8,112,384]{2,1,0:T(8,128)(2,1)S(1)} %slice.293), channel_id=1, source_target_pairs={{0,4},{1,5},{2,6},{3,7},{4,0},{5,1},{6,2},{7,3},{8,12},{9,13},{10,... | collective-permute-start | bytes 2064392 | tf_op jit(solution)/shard_map/ppermute | solution.py:474
  276.1 2.2 copy-start.1
  276.5 16.7 %collective-permute-start.28 = (bf16[8,112,384]{2,1,0:T(8,128)(2,1)S(1)}, bf16[8,112,384]{2,1,0:T(8,128)(2,1)S(1)}, u32[]{:S(2)}, u32[]{:S(2)}) collective-permute-start(bf16[8,112,384]{2,1,0:T(8,128)(2,1)S(1)} %slice.299), channel_id=1, source_target_pairs={{0,2},{1,3},{2,0},{3,1},{4,6},{5,7},{6,4},{7,5},{8,10},{9,11},{10,... | collective-permute-start | bytes 2064392 | tf_op jit(solution)/shard_map/ppermute | solution.py:474
  289.1 11.2 %collective-permute-start.26 = (bf16[4,112,384]{2,1,0:T(8,128)(2,1)S(1)}, bf16[4,112,384]{2,1,0:T(8,128)(2,1)S(1)}, u32[]{:S(2)}, u32[]{:S(2)}) collective-permute-start(bf16[4,112,384]{2,1,0:T(8,128)(2,1)S(1)} %slice.295), channel_id=1, source_target_pairs={{0,2},{1,3},{2,0},{3,1},{4,6},{5,7},{6,4},{7,5},{8,10},{9,11},{10,... | collective-permute-start | bytes 1032200 | tf_op jit(solution)/shard_map/ppermute | solution.py:474
  293.5 8.3 %collective-permute-start.29 = (bf16[4,112,384]{2,1,0:T(8,128)(2,1)S(1)}, bf16[4,112,384]{2,1,0:T(8,128)(2,1)S(1)}, u32[]{:S(2)}, u32[]{:S(2)}) collective-permute-start(bf16[4,112,384]{2,1,0:T(8,128)(2,1)S(1)} %slice.301), channel_id=1, source_target_pairs={{0,4},{1,5},{2,6},{3,7},{4,0},{5,1},{6,2},{7,3},{8,12},{9,13},{10,... | collective-permute-start | bytes 1032200 | tf_op jit(solution)/shard_map/ppermute | solution.py:474
  301.9 9.9 %collective-permute-start.30 = (bf16[224,384]{1,0:T(8,128)(2,1)S(1)}, bf16[224,384]{1,0:T(8,128)(2,1)S(1)}, u32[]{:S(2)}, u32[]{:S(2)}) collective-permute-start(bf16[224,384]{1,0:T(8,128)(2,1)S(1)} %get-tuple-element.72), channel_id=1, source_target_pairs={{0,8},{1,9},{2,10},{3,11},{4,12},{5,13},{6,14},{7,15},{8,0},{9,1},... | collective-permute-start | bytes 516104 | tf_op jit(solution)/shard_map/ppermute | solution.py:474
  303.5 9.4 %collective-permute-start.32 = (bf16[224,384]{1,0:T(8,128)(2,1)S(1)}, bf16[224,384]{1,0:T(8,128)(2,1)S(1)}, u32[]{:S(2)}, u32[]{:S(2)}) collective-permute-start(bf16[224,384]{1,0:T(8,128)(2,1)S(1)} %get-tuple-element.73), channel_id=1, source_target_pairs={{0,24},{1,25},{2,26},{3,27},{4,28},{5,29},{6,30},{7,31},{8,16},{9,... | collective-permute-start | bytes 516104 | tf_op jit(solution)/shard_map/ppermute | solution.py:474
  304.0 14.3 %collective-permute-start.31 = (bf16[224,384]{1,0:T(8,128)(2,1)S(1)}, bf16[224,384]{1,0:T(8,128)(2,1)S(1)}, u32[]{:S(2)}, u32[]{:S(2)}) collective-permute-start(bf16[224,384]{1,0:T(8,128)(2,1)S(1)} %get-tuple-element.74), channel_id=1, source_target_pairs={{0,16},{1,17},{2,18},{3,19},{4,20},{5,21},{6,22},{7,23},{8,24},{9,... | collective-permute-start | bytes 516104 | tf_op jit(solution)/shard_map/ppermute | solution.py:474
where the time goes:
time: 320 us; the launch traced here: 321 us
  starting transfers between devices  116 us (36%)
  waiting for transfers between devices  83.4 us (26%)
  Pallas kernels  78.1 us (24%)
  local copies, waits for them, and re-layouts  19.1 us (6%)
  other arithmetic  15.6 us (5%)
  matrix products  6.94 us (2%)
    ppermute x40, starting transfers between devices, permute(): return lax.ppermute(v, AXIS, [(i, i ^ mask) for i in range(size)])  116 us
    ppermute x40, waiting for transfers between devices, permute(): return lax.ppermute(v, AXIS, [(i, i ^ mask) for i in range(size)])  83.4 us
    pallas_call x1, Pallas kernels, run_middle(): pl.pallas_call(body, grid_spec=pltpu.PrefetchScalarGridSpec(num_scalar_pr...  33.1 us
    pallas_call x1, Pallas kernels, run_backward(): pl.pallas_call(body, grid_spec=pltpu.PrefetchScalarGridSpec(num_scalar_pr...  26.9 us
    pallas_call x1, Pallas kernels, run_forward(): pl.pallas_call(body, grid_spec=pltpu.PrefetchScalarGridSpec(num_scalar_pr...  18.1 us
    unnamed x38, local copies, waits for them, and re-layouts  8.84 us
  transfers between devices with their start and end apart: 40, of which 19 were waited for; matrix products, arithmetic and copies ran while one was open for 8% of the time, Pallas kernels for 14%

commit v1 on v0

--- a/solution.py
+++ b/solution.py
@@ -4,6 +4,7 @@
 from jax.experimental import pallas as pl
 from jax.experimental.pallas import tpu as pltpu
 from jax.sharding import PartitionSpec as P
+
 
 HEADS = 6
 D = 384
@@ -12,7 +13,6 @@
 BF = jnp.bfloat16
 F32 = jnp.float32
 SPLIT = 112
-PAYLOAD = 224
 BLOCKS = 32
 ROWS = 144
 AXIS = "fsdp"
@@ -212,7 +212,7 @@
     return jnp.concatenate([jnp.where(sub < 64, pair, zero), jnp.where(sub >= 64, pair, zero)], axis=1)
 
 
-def fetch_weights(table, pieces, wv, sem):
+def fetch_weights(table, pieces, wv, sem, clear=()):
     copies = []
     for ref, (masks, low, rows) in pieces:
         for k, mask in enumerate(masks):
@@ -224,6 +224,8 @@
             )
     for copy in copies:
         copy.start()
+    for ref in clear:
+        ref[...] = jnp.zeros_like(ref)
     for copy in copies:
         copy.wait()
 
@@ -316,9 +318,7 @@
 
         @pl.when(step == 0)
         def _():
-            fetch_weights(table_ref, list(zip(piece_refs, layout)), wv, sem)
-            for ref in acc + (dbias_ref, dmod_ref):
-                ref[...] = jnp.zeros_like(ref)
+            fetch_weights(table_ref, list(zip(piece_refs, layout)), wv, sem, acc + (dbias_ref, dmod_ref))
 
         @pl.when(step < table_ref[BLOCKS])
         def _():
@@ -399,9 +399,7 @@
 
         @pl.when(step == 0)
         def _():
-            fetch_weights(table_ref, list(zip(piece_refs, layout)), wv, sem)
-            for ref in acc + (dbias_ref, dmod_ref):
-                ref[...] = jnp.zeros_like(ref)
+            fetch_weights(table_ref, list(zip(piece_refs, layout)), wv, sem, acc + (dbias_ref, dmod_ref))
 
         @pl.when(step < table_ref[BLOCKS])
         def _():
@@ -549,9 +547,15 @@
     return added(keep1, permute(send1, 1)).astype(BF), added(keep2, permute(send2, 1)).astype(BF)
 
 
-def reduce_rest(one, two):
-    one = added(one[:8], permute(one[8:], 4)).astype(BF)
-    two = added(two[:8], permute(two[8:], 2)).astype(BF)
+def reduce_near(one, two):
+    from_one = permute(one[8:], 4)
+    from_two = permute(two[8:], 2)
+    return from_one, from_two
+
+
+def reduce_rest(one, two, near):
+    one = added(one[:8], near[0]).astype(BF)
+    two = added(two[:8], near[1]).astype(BF)
     one = added(one[:4], permute(one[4:], 2)).astype(BF)
     two = added(two[:4], permute(two[4:], 4)).astype(BF)
     both = jnp.concatenate([one, two], axis=1)
@@ -564,7 +568,7 @@
     return (masks[None, :] ^ me) == jnp.arange(BLOCKS, dtype=jnp.int32)[:, None]
 
 
-def per_device(
+def whole_step(
     latents, cond, live_counts, ada_weight, attn_weight, mlp_in, mlp_out, bias_all, cotangent
 ):
     slots = latents.shape[0]
@@ -594,7 +598,10 @@
 
     def modulation(ada, bias):
         bias = bias.reshape(-1).astype(F32)
-        modulate = jnp.einsum("sd,jed->sje", cond_low, ada, preferred_element_type=F32)
+        modulate = [
+            jnp.einsum("sd,jed->sje", cond_low, part, preferred_element_type=F32) for part in ada
+        ]
+        modulate = jnp.concatenate(modulate, axis=1)
         if fast:
             modulate = jnp.einsum(
                 "jp,spe->sje", rank.astype(F32), modulate, precision=lax.Precision.HIGHEST
@@ -602,18 +609,19 @@
         return bias[None, 6 * D :], modulate.reshape(slots, 6 * D) + bias[: 6 * D]
 
     def unpack_fast(one, two):
-        full = jnp.concatenate([p[:, ROWS - SPLIT :] for p in two], axis=0)
-        ada = full[:, :ada_rows]
-        bias = jnp.dot(rank.astype(BF), full[:, ada_rows, :bias_count], preferred_element_type=F32)
+        base = ROWS - SPLIT
+        ada = [p[:, base : base + ada_rows] for p in two]
+        bias = jnp.concatenate([p[:, base + ada_rows, :bias_count] for p in two], axis=0)
+        bias = jnp.dot(rank.astype(BF), bias, preferred_element_type=F32)
         return (one + two, ada) + modulation(ada, bias)
 
     def unpack_plain(full):
         parts = [full[:, k * attn_rows : (k + 1) * attn_rows].reshape(BLOCKS, 48, D) for k in range(3)]
-        ada = full[:, 3 * attn_rows : 3 * attn_rows + ada_rows].reshape(BLOCKS, -1, D)
+        ada = [full[:, 3 * attn_rows : 3 * attn_rows + ada_rows].reshape(BLOCKS, -1, D)]
         bias = full[:, 3 * attn_rows + ada_rows, :bias_count]
         return ([jnp.concatenate(parts, axis=1)], ada) + modulation(ada, bias)
 
-    def local_grads(layer, result, ada):
+    def local_grads(result, ada):
         grad_modulate, grad_bias = result[:2]
         grad_low = grad_modulate.astype(BF)
         bias_full = jnp.concatenate([jnp.sum(grad_low.astype(F32), axis=0), grad_bias[0]])
@@ -624,7 +632,10 @@
                 "jp,sje->spe", rank.astype(BF), grouped, preferred_element_type=F32
             ).astype(BF)
             bias_rows = jnp.einsum("jp,je->pe", rank.astype(BF), bias_rows, preferred_element_type=F32)
-        cond_part = jnp.einsum("sje,jed->sd", grouped, ada, preferred_element_type=F32)
+        cond_part = 0.0
+        for k, part in enumerate(ada):
+            chunk = grouped[:, k * part.shape[0] : (k + 1) * part.shape[0]]
+            cond_part = cond_part + jnp.einsum("sje,jed->sd", chunk, part, preferred_element_type=F32)
         ada_grad = jnp.einsum("sje,sd->jed", grouped, cond_low, preferred_element_type=F32)
         tail = jnp.pad(bias_rows[:, None], ((0, 0), (0, 7 if fast else 0), (0, D - bias_count)))
         if fast:
@@ -646,7 +657,9 @@
         far0 = (permute(near0[0], 4), permute(near0[1], 2))
         near1 = gather_near(tie(line1, *far0))
         block0 = unpack_fast(*gather_rest(near0, far0))
-        far1 = (permute(near1[0], 4), permute(near1[1], 2))
+        far_one = permute(near1[0], 4)
+        far_two = permute(near1[1], 2)
+        far1 = (far_one, far_two)
         first_table = tie(table, *near1)
     else:
         full = [lax.all_gather(payload(layer), AXIS, axis=0, tiled=False) for layer in range(layers)]
@@ -661,24 +674,25 @@
         table, saved[7], cotangent, block1[3], block1[2], block1[0], layout, orders
     )
     output, upstream = middle[:2]
-    cond_part, extra = local_grads(1, middle[2:], block1[1])
+    cond_part, extra = local_grads(middle[2:], block1[1])
     cond_grad = cond_grad + cond_part
     last_table = table
     if fast:
         one1, two1 = reduce_core(middle[4:], extra)
         last_table = tie(table, one1, two1)
+        reduced1 = reduce_near(one1, two1)
     else:
         shards[1] = lax.psum_scatter(extra, AXIS, scatter_dimension=0, tiled=False)
     last = run_backward(
         last_table, latents, upstream, block0[3], block0[0], layout, saved[:7], orders
     )
     grad_latents = last[0]
-    cond_part, extra = local_grads(0, last[1:], block0[1])
+    cond_part, extra = local_grads(last[1:], block0[1])
     cond_grad = cond_grad + cond_part
     if fast:
         one0, two0 = reduce_core(last[3:], extra)
-        shards[1] = reduce_rest(one1, two1)
-        shards[0] = reduce_rest(one0, two0)
+        shards[1] = reduce_rest(one1, two1, reduced1)
+        shards[0] = reduce_rest(one0, two0, reduce_near(one0, two0))
     else:
         shards[0] = lax.psum_scatter(extra, AXIS, scatter_dimension=0, tiled=False)
     cond_grad = cond_grad * silu_slope(cond_value)
@@ -704,7 +718,7 @@
     column = P(None, None, "fsdp")
     row = P(None, "fsdp", None)
     return jax.shard_map(
-        per_device,
+        whole_step,
         mesh=mesh,
         in_specs=(token, P("fsdp", None), P("fsdp"), column, column, column, row, P(None, "fsdp"), token),
         out_specs=(token, token, P("fsdp", None), column, column, column, row, P(None, "fsdp")),

time: 320 us -> 317 us (level)
  starting transfers between devices: 116 us -> 101 us
  waiting for transfers between devices: 83.4 us -> 97.2 us
  local copies, waits for them, and re-layouts: 19.1 us -> 13.7 us
  matrix products: 6.94 us -> 12.2 us
    ppermute x40, starting transfers between devices: 116 us -> 101 us  [permute(): return lax.ppermute(v, AXIS, [(i, i ^ mask) for i in range(size)])]
    ppermute x40, waiting for transfers between devices: 83.4 us -> 97.2 us  [permute(): return lax.ppermute(v, AXIS, [(i, i ^ mask) for i in range(size)])]
    dot_general x6 -> x18, matrix products: 4.11 us -> 9.44 us  [the longest x8 4.49 us: local_grads(): jnp.einsum('sje,jed->sd', chunk, part, preferred_element_type=F32)]
    slice x12 -> x14, local copies, waits for them, and re-layouts: 6.5 us -> 3.72 us  [the longest x6 1.62 us: unpack_fast(): p[:, base + ada_rows, :bias_count]]
    unnamed x38 -> x66, local copies, waits for them, and re-layouts: 8.84 us -> 6.18 us
  transfers between devices with their start and end apart: 40 -> 40, of which waited for: 19 -> 22; matrix products, arithmetic and copies ran while one was open for 8% -> 7% of each run, Pallas kernels for 14% -> 6%
where the time goes in v1:
time: 317 us; the launch traced here: 316 us
  starting transfers between devices  101 us (32%)
  waiting for transfers between devices  97.2 us (31%)
  Pallas kernels  77.4 us (24%)
  local copies, waits for them, and re-layouts  13.7 us (4%)
  other arithmetic  12.6 us (4%)
  matrix products  12.2 us (4%)
    ppermute x40, starting transfers between devices, permute(): return lax.ppermute(v, AXIS, [(i, i ^ mask) for i in range(size)])  101 us
    ppermute x40, waiting for transfers between devices, permute(): return lax.ppermute(v, AXIS, [(i, i ^ mask) for i in range(size)])  97.2 us
    pallas_call x1, Pallas kernels, run_middle(): pl.pallas_call(body, grid_spec=pltpu.PrefetchScalarGridSpec(num_scalar_pr...  32.7 us
    pallas_call x1, Pallas kernels, run_backward(): pl.pallas_call(body, grid_spec=pltpu.PrefetchScalarGridSpec(num_scalar_pr...  26.5 us
    pallas_call x1, Pallas kernels, run_forward(): pl.pallas_call(body, grid_spec=pltpu.PrefetchScalarGridSpec(num_scalar_pr...  18.1 us
  transfers between devices with their start and end apart: 40, of which 22 were waited for; matrix products, arithmetic and copies ran while one was open for 7% of the time, Pallas kernels for 6%

profile of v1, /device:TPU:0, one launch (start us, length us, event | category | flops | bytes accessed | tf_op | source)
XLA Modules:
  0.0 315.7 jit_solution(8928221159912953687)
XLA Ops:
  0.6 0.8 slice_reduce_fusion
  1.4 0.8 bitcast_dynamic-update-slice_fusion.3
  2.2 0.8 bitcast_dynamic-update-slice_fusion.2
  3.0 0.8 bitcast_dynamic-update-slice_fusion.6
  3.8 0.9 bitcast_dynamic-update-slice_fusion
  4.7 5.1 %collective-permute-start.2 = (bf16[224,384]{1,0:T(8,128)(2,1)S(1)}, bf16[224,384]{1,0:T(8,128)(2,1)S(1)}, u32[]{:S(2)}, u32[]{:S(2)}) collective-permute-start(bf16[224,384]{1,0:T(8,128)(2,1)S(1)} %constant_dynamic-update-slice_fusion.1), channel_id=1, source_target_pairs={{0,24},{1,25},{2,26},{3,27},{4,28},{5,29},{6,30},{7,31},{8,16},{9,... | collective-permute-start | bytes 516104 | tf_op jit(solution)/shard_map/ppermute | solution.py:472
  10.5 4.7 %collective-permute-done.2 = bf16[224,384]{1,0:T(8,128)(2,1)S(1)} collective-permute-done((bf16[224,384]{1,0:T(8,128)(2,1)S(1)}, bf16[224,384]{1,0:T(8,128)(2,1)S(1)}, u32[]{:S(2)}, u32[]{:S(2)}) %collective-permute-start.2) | collective-permute-done | bytes 172064 | tf_op jit(solution)/shard_map/ppermute | solution.py:472
  15.2 9.3 %collective-permute-done.1 = bf16[224,384]{1,0:T(8,128)(2,1)S(1)} collective-permute-done((bf16[224,384]{1,0:T(8,128)(2,1)S(1)}, bf16[224,384]{1,0:T(8,128)(2,1)S(1)}, u32[]{:S(2)}, u32[]{:S(2)}) %collective-permute-start.1) | collective-permute-done | bytes 172064 | tf_op jit(solution)/shard_map/ppermute | solution.py:472
  24.6 1.6 collective-permute-start.8
  26.9 1.6 collective-permute-start.6
  28.5 2.5 collective-permute-start.5
  31.0 1.9 collective-permute-start.3
  32.9 1.0 collective-permute-done.8
  33.9 1.6 collective-permute-start.9
  35.5 1.3 collective-permute-done.6
  37.8 6.3 %collective-permute-done.4 = bf16[224,384]{1,0:T(8,128)(2,1)S(1)} collective-permute-done((bf16[224,384]{1,0:T(8,128)(2,1)S(1)}, bf16[224,384]{1,0:T(8,128)(2,1)S(1)}, u32[]{:S(2)}, u32[]{:S(2)}) %collective-permute-start.4) | collective-permute-done | bytes 172064 | tf_op jit(solution)/shard_map/ppermute | solution.py:472
  45.2 5.4 %collective-permute-done.9.rest_5_.rest_12_ = bf16[8,112,384]{2,1,0:T(8,128)(2,1)S(1)} collective-permute-done((bf16[8,112,384]{2,1,0:T(8,128)(2,1)S(1)}, bf16[8,112,384]{2,1,0:T(8,128)(2,1)S(1)}, u32[]{:S(2)}, u32[]{:S(2)}) %collective-permute-start.9) | collective-permute-done | bytes 688160 | tf_op jit(solution)/shard_map/ppermute | solution.py:472
  50.6 0.8 collective-permute-done.7.rest_1_.rest_8_
  51.5 1.6 collective-permute-start.10
  54.8 5.5 %collective-permute-done.11 = bf16[4,112,384]{2,1,0:T(8,128)(2,1)S(1)} collective-permute-done((bf16[4,112,384]{2,1,0:T(8,128)(2,1)S(1)}, bf16[4,112,384]{2,1,0:T(8,128)(2,1)S(1)}, u32[]{:S(2)}, u32[]{:S(2)}) %collective-permute-start.11) | collective-permute-done | bytes 344096 | tf_op jit(solution)/shard_map/ppermute | solution.py:472
  64.3 1.1 collective-permute-start.19
  65.4 13.1 %collective-permute-done.16.rest_5_ = bf16[8,112,384]{2,1,0:T(8,128)(2,1)} collective-permute-done((bf16[8,112,384]{2,1,0:T(8,128)(2,1)S(1)}, bf16[8,112,384]{2,1,0:T(8,128)(2,1)}, u32[]{:S(2)}, u32[]{:S(2)}) %collective-permute-start.16) | collective-permute-done | bytes 688160 | tf_op jit(solution)/shard_map/ppermute | solution.py:472
  78.5 18.1 %forward_zero.1 = (bf16[7,256,1152]{2,1,0:T(8,128)(2,1)}, bf16[7,256,1536]{2,1,0:T(8,128)(2,1)}, bf16[7,256,384]{2,1,0:T(8,128)(2,1)}, f32[7,256,384]{2,1,0:T(8,...) custom-call(s32[33]{0:T(128)} %pad_add_fusion.table_ref, ...), custom_call_target="tpu_custom_call" | custom-call | flops 7699999744 | bytes 40000000 | tf_op jit(solution)/shard_map/forward_zero/pallas_call | solution.py:277
  96.7 0.8 slice.342
  98.2 4.1 %collective-permute-start.21 = (bf16[8,112,384]{2,1,0:T(8,128)(2,1)}, bf16[8,112,384]{2,1,0:T(8,128)(2,1)S(1)}, u32[]{:S(2)}, u32[]{:S(2)}) collective-permute-start(bf16[8,112,384]{2,1,0:T(8,128)(2,1)} %collective-permute-done.19.rest_1_), channel_id=1, source_target_pairs={{0,1},{1,0},{2,3},{3,2},{4,5},{5,4},{6,7},{7,6},{8,9},{9,8},{10,11... | collective-permute-start | bytes 2064392 | tf_op jit(solution)/shard_map/ppermute | solution.py:472
  102.4 1.3 fusion.22
  103.7 1.3 fusion.25
  107.5 0.9 copy-done.25
  108.3 32.7 %middle_one.1 = (bf16[7,256,384]{2,1,0:T(8,128)(2,1)}, f32[7,256,384]{2,1,0:T(8,128)}, f32[7,2304]{1,0:T(8,128)}, f32[1,3072]{1,0:T(1,128)}, bf16[16,112,384]{2,...) custom-call(s32[33]{0:T(128)} %pad_add_fusion.table_ref, ...), custom_call_target="tpu_custom_call" | custom-call | flops 23100000256 | bytes 20000000 | tf_op jit(solution)/shard_map/middle_one/pallas_call | solution.py:344
  141.8 0.9 fusion.119
  143.5 7.2 %collective-permute-start.22 = (bf16[16,112,384]{2,1,0:T(8,128)(2,1)}, bf16[16,112,384]{2,1,0:T(8,128)(2,1)S(1)}, u32[]{:S(2)}, u32[]{:S(2)}) collective-permute-start(bf16[16,112,384]{2,1,0:T(8,128)(2,1)} %get-tuple-element.41), channel_id=1, source_target_pairs={{0,1},{1,0},{2,3},{3,2},{4,5},{5,4},{6,7},{7,6},{8,9},{9,8},{10,11... | collective-permute-start | bytes 4128776 | tf_op jit(solution)/shard_map/ppermute | solution.py:472
  151.8 0.8 copy-done.11
  152.8 1.4 convolution_bitcast_fusion.8
  154.4 1.2 fusion.14
  156.1 1.0 slice.374
  157.8 0.9 slice.378
  158.7 26.5 %backward_zero.1 = (f32[7,256,384]{2,1,0:T(8,128)}, f32[7,2304]{1,0:T(8,128)}, f32[1,3072]{1,0:T(1,128)}, bf16[16,112,384]{2,1,0:T(8,128)(2,1)}, bf16[16,112,384...) custom-call(s32[33]{0:T(128)} %pad_add_fusion.table_ref, bf16[7,256,384]{2,1,0:T(8,128)(2,1)} %lat_ref.3, ...), custom_call_target="tpu_custom_call" | custom-call | flops 15399999488 | bytes 50000000 | tf_op jit(solution)/shard_map/backward_zero/pallas_call | solution.py:431
  185.2 0.9 fusion.118
  187.2 52.3 %collective-permute-start.33 = (bf16[8,112,384]{2,1,0:T(8,128)(2,1)}, bf16[8,112,384]{2,1,0:T(8,128)(2,1)}, u32[]{:S(2)}, u32[]{:S(2)}) collective-permute-start(bf16[8,112,384]{2,1,0:T(8,128)(2,1)} %slice.374), channel_id=1, source_target_pairs={{0,4},{1,5},{2,6},{3,7},{4,0},{5,1},{6,2},{7,3},{8,12},{9,13},{10,... | collective-permute-start | bytes 2064392 | tf_op jit(solution)/shard_map/ppermute | solution.py:472
  239.9 1.3 collective-permute-start.35
  243.8 11.8 %collective-permute-done.33 = bf16[8,112,384]{2,1,0:T(8,128)(2,1)} collective-permute-done((bf16[8,112,384]{2,1,0:T(8,128)(2,1)}, bf16[8,112,384]{2,1,0:T(8,128)(2,1)}, u32[]{:S(2)}, u32[]{:S(2)}) %collective-permute-start.33) | collective-permute-done | bytes 688160 | tf_op jit(solution)/shard_map/ppermute | solution.py:472
  255.6 1.3 add_convert_fusion.5
  256.9 1.8 collective-permute-start.34
  258.9 1.3 collective-permute-start.36
  260.5 6.5 %collective-permute-done.34 = bf16[4,112,384]{2,1,0:T(8,128)(2,1)S(1)} collective-permute-done((bf16[4,112,384]{2,1,0:T(8,128)(2,1)S(1)}, bf16[4,112,384]{2,1,0:T(8,128)(2,1)S(1)}, u32[]{:S(2)}, u32[]{:S(2)}) %collective-permute-start.34) | collective-permute-done | bytes 344096 | tf_op jit(solution)/shard_map/ppermute | solution.py:472
  267.1 1.7 collective-permute-done.36
  269.0 1.7 collective-permute-start.39
  270.7 1.7 collective-permute-start.38
  273.9 0.9 collective-permute-start.28
  274.8 0.8 fusion.13
  275.7 1.1 collective-permute-done.37
  276.8 2.7 collective-permute-done.39
  279.5 7.0 %collective-permute-done.38 = bf16[224,384]{1,0:T(8,128)(2,1)S(1)} collective-permute-done((bf16[224,384]{1,0:T(8,128)(2,1)S(1)}, bf16[224,384]{1,0:T(8,128)(2,1)S(1)}, u32[]{:S(2)}, u32[]{:S(2)}) %collective-permute-start.38) | collective-permute-done | bytes 172064 | tf_op jit(solution)/shard_map/ppermute | solution.py:472
  286.5 1.9 collective-permute-done.25
  289.1 1.2 collective-permute-done.28
  290.5 2.5 collective-permute-start.29
  293.1 3.7 %collective-permute-done.26 = bf16[4,112,384]{2,1,0:T(8,128)(2,1)S(1)} collective-permute-done((bf16[4,112,384]{2,1,0:T(8,128)(2,1)S(1)}, bf16[4,112,384]{2,1,0:T(8,128)(2,1)S(1)}, u32[]{:S(2)}, u32[]{:S(2)}) %collective-permute-start.26) | collective-permute-done | bytes 344096 | tf_op jit(solution)/shard_map/ppermute | solution.py:472
  296.9 1.4 collective-permute-done.29
  298.5 1.0 collective-permute-start.30
  299.5 1.5 collective-permute-start.32
  301.0 1.0 collective-permute-start.31
  302.0 2.5 collective-permute-done.30
  304.5 2.8 collective-permute-done.32
  307.3 5.6 %collective-permute-done.31 = bf16[224,384]{1,0:T(8,128)(2,1)S(1)} collective-permute-done((bf16[224,384]{1,0:T(8,128)(2,1)S(1)}, bf16[224,384]{1,0:T(8,128)(2,1)S(1)}, u32[]{:S(2)}, u32[]{:S(2)}) %collective-permute-start.31) | collective-permute-done | bytes 172064 | tf_op jit(solution)/shard_map/ppermute | solution.py:472
  (205 shorter events, 26.1 us)
Async XLA Ops:
  0.6 27.9 %copy-start.26 = (s32[32]{0:T(128)S(1)}, s32[32]{0:T(128)}, u32[]{:S(2)}) copy-start(s32[32]{0:T(128)} %constant.15.clone) | copy-start | bytes 388
  4.7 10.5 %collective-permute-start.2 = (bf16[224,384]{1,0:T(8,128)(2,1)S(1)}, bf16[224,384]{1,0:T(8,128)(2,1)S(1)}, u32[]{:S(2)}, u32[]{:S(2)}) collective-permute-start(bf16[224,384]{1,0:T(8,128)(2,1)S(1)} %constant_dynamic-update-slice_fusion.1), channel_id=1, source_target_pairs={{0,24},{1,25},{2,26},{3,27},{4,28},{5,29},{6,30},{7,31},{8,16},{9,... | collective-permute-start | bytes 516104 | tf_op jit(solution)/shard_map/ppermute | solution.py:472
  9.9 14.6 %collective-permute-start.1 = (bf16[224,384]{1,0:T(8,128)(2,1)S(1)}, bf16[224,384]{1,0:T(8,128)(2,1)S(1)}, u32[]{:S(2)}, u32[]{:S(2)}) collective-permute-start(bf16[224,384]{1,0:T(8,128)(2,1)S(1)} %constant_dynamic-update-slice_fusion.1), channel_id=1, source_target_pairs={{0,16},{1,17},{2,18},{3,19},{4,20},{5,21},{6,22},{7,23},{8,24},{9,... | collective-permute-start | bytes 516104 | tf_op jit(solution)/shard_map/ppermute | solution.py:472
  9.9 14.6 %collective-permute-start = (bf16[224,384]{1,0:T(8,128)(2,1)S(1)}, bf16[224,384]{1,0:T(8,128)(2,1)S(1)}, u32[]{:S(2)}, u32[]{:S(2)}) collective-permute-start(bf16[224,384]{1,0:T(8,128)(2,1)S(1)} %constant_dynamic-update-slice_fusion.1), channel_id=1, source_target_pairs={{0,8},{1,9},{2,10},{3,11},{4,12},{5,13},{6,14},{7,15},{8,0},{9,1},... | collective-permute-start | bytes 516104 | tf_op jit(solution)/shard_map/ppermute | solution.py:472
  24.6 9.2 %collective-permute-start.8 = (bf16[4,112,384]{2,1,0:T(8,128)(2,1)S(1)}, bf16[4,112,384]{2,1,0:T(8,128)(2,1)S(1)}, u32[]{:S(2)}, u32[]{:S(2)}) collective-permute-start(bf16[4,112,384]{2,1,0:T(8,128)(2,1)S(1)} %get-tuple-element.80), channel_id=1, source_target_pairs={{0,4},{1,5},{2,6},{3,7},{4,0},{5,1},{6,2},{7,3},{8,12},{9,13},{10,... | collective-permute-start | bytes 1032200 | tf_op jit(solution)/shard_map/ppermute | solution.py:472
  26.9 9.9 %collective-permute-start.6 = (bf16[4,112,384]{2,1,0:T(8,128)(2,1)S(1)}, bf16[4,112,384]{2,1,0:T(8,128)(2,1)S(1)}, u32[]{:S(2)}, u32[]{:S(2)}) collective-permute-start(bf16[4,112,384]{2,1,0:T(8,128)(2,1)S(1)} %get-tuple-element.81), channel_id=1, source_target_pairs={{0,2},{1,3},{2,0},{3,1},{4,6},{5,7},{6,4},{7,5},{8,10},{9,11},{10,... | collective-permute-start | bytes 1032200 | tf_op jit(solution)/shard_map/ppermute | solution.py:472
  28.5 9.3 %collective-permute-start.5 = (bf16[224,384]{1,0:T(8,128)(2,1)S(1)}, bf16[224,384]{1,0:T(8,128)(2,1)S(1)}, u32[]{:S(2)}, u32[]{:S(2)}) collective-permute-start(bf16[224,384]{1,0:T(8,128)(2,1)S(1)} %constant_dynamic-update-slice_fusion), channel_id=1, source_target_pairs={{0,24},{1,25},{2,26},{3,27},{4,28},{5,29},{6,30},{7,31},{8,16},{9,... | collective-permute-start | bytes 516104 | tf_op jit(solution)/shard_map/ppermute | solution.py:472
  31.0 13.1 %collective-permute-start.4 = (bf16[224,384]{1,0:T(8,128)(2,1)S(1)}, bf16[224,384]{1,0:T(8,128)(2,1)S(1)}, u32[]{:S(2)}, u32[]{:S(2)}) collective-permute-start(bf16[224,384]{1,0:T(8,128)(2,1)S(1)} %constant_dynamic-update-slice_fusion), channel_id=1, source_target_pairs={{0,16},{1,17},{2,18},{3,19},{4,20},{5,21},{6,22},{7,23},{8,24},{9,... | collective-permute-start | bytes 516104 | tf_op jit(solution)/shard_map/ppermute | solution.py:472
  31.0 13.1 %collective-permute-start.3 = (bf16[224,384]{1,0:T(8,128)(2,1)S(1)}, bf16[224,384]{1,0:T(8,128)(2,1)S(1)}, u32[]{:S(2)}, u32[]{:S(2)}) collective-permute-start(bf16[224,384]{1,0:T(8,128)(2,1)S(1)} %constant_dynamic-update-slice_fusion), channel_id=1, source_target_pairs={{0,8},{1,9},{2,10},{3,11},{4,12},{5,13},{6,14},{7,15},{8,0},{9,1},... | collective-permute-start | bytes 516104 | tf_op jit(solution)/shard_map/ppermute | solution.py:472
  33.9 10.9 %copy-start.6 = (bf16[8,112,384]{2,1,0:T(8,128)(2,1)}, bf16[8,112,384]{2,1,0:T(8,128)(2,1)S(1)}, u32[]{:S(2)}) copy-start(bf16[8,112,384]{2,1,0:T(8,128)(2,1)S(1)} %pad_maximum_fusion.2.rest_4_.rest_11_) | copy-start | bytes 2064388
  33.9 16.7 %collective-permute-start.9 = (bf16[8,112,384]{2,1,0:T(8,128)(2,1)S(1)}, bf16[8,112,384]{2,1,0:T(8,128)(2,1)S(1)}, u32[]{:S(2)}, u32[]{:S(2)}) collective-permute-start(bf16[8,112,384]{2,1,0:T(8,128)(2,1)S(1)} %pad_maximum_fusion.2.rest_4_.rest_11_), channel_id=1, source_target_pairs={{0,2},{1,3},{2,0},{3,1},{4,6},{5,7},{6,4},{7,5},{8,10},{9,11},{10,... | collective-permute-start | bytes 2064392 | tf_op jit(solution)/shard_map/ppermute | solution.py:472
  36.9 8.3 %copy-start.7 = (bf16[8,112,384]{2,1,0:T(8,128)(2,1)}, bf16[8,112,384]{2,1,0:T(8,128)(2,1)S(1)}, u32[]{:S(2)}) copy-start(bf16[8,112,384]{2,1,0:T(8,128)(2,1)S(1)} %pad_maximum_fusion.6.rest_0_.rest_7_) | copy-start | bytes 2064388
  36.9 8.0 %copy-start.20 = (bf16[7,384]{1,0:T(8,128)(2,1)S(1)}, bf16[7,384]{1,0:T(8,128)(2,1)}, u32[]{:S(2)}) copy-start(bf16[7,384]{1,0:T(8,128)(2,1)} %param.11) | copy-start | bytes 16132
  36.9 14.5 %collective-permute-start.7 = (bf16[8,112,384]{2,1,0:T(8,128)(2,1)S(1)}, bf16[8,112,384]{2,1,0:T(8,128)(2,1)S(1)}, u32[]{:S(2)}, u32[]{:S(2)}) collective-permute-start(bf16[8,112,384]{2,1,0:T(8,128)(2,1)S(1)} %pad_maximum_fusion.6.rest_0_.rest_7_), channel_id=1, source_target_pairs={{0,4},{1,5},{2,6},{3,7},{4,0},{5,1},{6,2},{7,3},{8,12},{9,13},{10,... | collective-permute-start | bytes 2064392 | tf_op jit(solution)/shard_map/ppermute | solution.py:472
  44.2 9.6 %collective-permute-start.12 = (bf16[8,112,384]{2,1,0:T(8,128)(2,1)S(1)}, bf16[8,112,384]{2,1,0:T(8,128)(2,1)S(1)}, u32[]{:S(2)}, u32[]{:S(2)}) collective-permute-start(bf16[8,112,384]{2,1,0:T(8,128)(2,1)S(1)} %pad_maximum_fusion.2.rest_4_.rest_11_), channel_id=1, source_target_pairs={{0,1},{1,0},{2,3},{3,2},{4,5},{5,4},{6,7},{7,6},{8,9},{9,8},{10,11... | collective-permute-start | bytes 2064392 | tf_op jit(solution)/shard_map/ppermute | solution.py:472
  44.3 20.0 %collective-permute-start.14 = (bf16[8,112,384]{2,1,0:T(8,128)(2,1)S(1)}, bf16[8,112,384]{2,1,0:T(8,128)(2,1)}, u32[]{:S(2)}, u32[]{:S(2)}) collective-permute-start(bf16[8,112,384]{2,1,0:T(8,128)(2,1)S(1)} %pad_maximum_fusion.6.rest_0_.rest_7_), channel_id=1, source_target_pairs={{0,1},{1,0},{2,3},{3,2},{4,5},{5,4},{6,7},{7,6},{8,9},{9,8},{10,11... | collective-permute-start | bytes 2064392 | tf_op jit(solution)/shard_map/ppermute | solution.py:472
  44.9 5.7 %copy-start.2 = (bf16[8,72,384]{2,1,0:T(8,128)(2,1)}, bf16[8,72,384]{2,1,0:T(8,128)(2,1)S(1)}, u32[]{:S(2)}) copy-start(bf16[8,72,384]{2,1,0:T(8,128)(2,1)S(1)} %fusion.17) | copy-start | bytes 1327108
  50.6 9.8 %copy-start.14 = (bf16[8,112,384]{2,1,0:T(8,128)(2,1)}, bf16[8,112,384]{2,1,0:T(8,128)(2,1)S(1)}, u32[]{:S(2)}) copy-start(bf16[8,112,384]{2,1,0:T(8,128)(2,1)S(1)} %collective-permute-done.9.rest_5_.rest_12_) | copy-start | bytes 2064388
  51.4 9.1 %copy-start.24 = (bf16[8,112,384]{2,1,0:T(8,128)(2,1)}, bf16[8,112,384]{2,1,0:T(8,128)(2,1)S(1)}, u32[]{:S(2)}) copy-start(bf16[8,112,384]{2,1,0:T(8,128)(2,1)S(1)} %collective-permute-done.7.rest_1_.rest_8_) | copy-start | bytes 2064388
  51.5 9.1 %collective-permute-start.10 = (bf16[4,112,384]{2,1,0:T(8,128)(2,1)S(1)}, bf16[4,112,384]{2,1,0:T(8,128)(2,1)S(1)}, u32[]{:S(2)}, u32[]{:S(2)}) collective-permute-start(bf16[4,112,384]{2,1,0:T(8,128)(2,1)S(1)} %get-tuple-element.79), channel_id=1, source_target_pairs={{0,2},{1,3},{2,0},{3,1},{4,6},{5,7},{6,4},{7,5},{8,10},{9,11},{10,... | collective-permute-start | bytes 1032200 | tf_op jit(solution)/shard_map/ppermute | solution.py:472
  53.0 7.3 %collective-permute-start.11 = (bf16[4,112,384]{2,1,0:T(8,128)(2,1)S(1)}, bf16[4,112,384]{2,1,0:T(8,128)(2,1)S(1)}, u32[]{:S(2)}, u32[]{:S(2)}) collective-permute-start(bf16[4,112,384]{2,1,0:T(8,128)(2,1)S(1)} %get-tuple-element.78), channel_id=1, source_target_pairs={{0,4},{1,5},{2,6},{3,7},{4,0},{5,1},{6,2},{7,3},{8,12},{9,13},{10,... | collective-permute-start | bytes 1032200 | tf_op jit(solution)/shard_map/ppermute | solution.py:472
  53.8 6.7 %copy-start.16 = (bf16[8,112,384]{2,1,0:T(8,128)(2,1)}, bf16[8,112,384]{2,1,0:T(8,128)(2,1)S(1)}, u32[]{:S(2)}) copy-start(bf16[8,112,384]{2,1,0:T(8,128)(2,1)S(1)} %collective-permute-done.12.rest_6_.rest_13_) | copy-start | bytes 2064388
  54.2 7.4 %collective-permute-start.13 = (bf16[8,112,384]{2,1,0:T(8,128)(2,1)S(1)}, bf16[8,112,384]{2,1,0:T(8,128)(2,1)S(1)}, u32[]{:S(2)}, u32[]{:S(2)}) collective-permute-start(bf16[8,112,384]{2,1,0:T(8,128)(2,1)S(1)} %collective-permute-done.9.rest_5_.rest_12_), channel_id=1, source_target_pairs={{0,1},{1,0},{2,3},{3,2},{4,5},{5,4},{6,7},{7,6},{8,9},{9,8},{10,11... | collective-permute-start | bytes 2064392 | tf_op jit(solution)/shard_map/ppermute | solution.py:472
  54.3 24.2 %collective-permute-start.15 = (bf16[8,112,384]{2,1,0:T(8,128)(2,1)S(1)}, bf16[8,112,384]{2,1,0:T(8,128)(2,1)}, u32[]{:S(2)}, u32[]{:S(2)}) collective-permute-start(bf16[8,112,384]{2,1,0:T(8,128)(2,1)S(1)} %collective-permute-done.7.rest_1_.rest_8_), channel_id=1, source_target_pairs={{0,1},{1,0},{2,3},{3,2},{4,5},{5,4},{6,7},{7,6},{8,9},{9,8},{10,11... | collective-permute-start | bytes 2064392 | tf_op jit(solution)/shard_map/ppermute | solution.py:472
  60.5 1.7 copy-start.8
  60.5 36.2 %collective-permute-start.17 = (bf16[8,112,384]{2,1,0:T(8,128)(2,1)S(1)}, bf16[8,112,384]{2,1,0:T(8,128)(2,1)}, u32[]{:S(2)}, u32[]{:S(2)}) collective-permute-start(bf16[8,112,384]{2,1,0:T(8,128)(2,1)S(1)} %pad_maximum_fusion.3.rest_4_), channel_id=1, source_target_pairs={{0,1},{1,0},{2,3},{3,2},{4,5},{5,4},{6,7},{7,6},{8,9},{9,8},{10,11... | collective-permute-start | bytes 2064392 | tf_op jit(solution)/shard_map/ppermute | solution.py:472
  60.6 17.9 %collective-permute-start.16 = (bf16[8,112,384]{2,1,0:T(8,128)(2,1)S(1)}, bf16[8,112,384]{2,1,0:T(8,128)(2,1)}, u32[]{:S(2)}, u32[]{:S(2)}) collective-permute-start(bf16[8,112,384]{2,1,0:T(8,128)(2,1)S(1)} %pad_maximum_fusion.3.rest_4_), channel_id=1, source_target_pairs={{0,2},{1,3},{2,0},{3,1},{4,6},{5,7},{6,4},{7,5},{8,10},{9,11},{10,... | collective-permute-start | bytes 2064392 | tf_op jit(solution)/shard_map/ppermute | solution.py:472
  61.3 35.4 %copy-start.9 = (bf16[8,112,384]{2,1,0:T(8,128)(2,1)}, bf16[8,112,384]{2,1,0:T(8,128)(2,1)S(1)}, u32[]{:S(2)}) copy-start(bf16[8,112,384]{2,1,0:T(8,128)(2,1)S(1)} %pad_maximum_fusion.7.rest_0_) | copy-start | bytes 2064388
  61.6 45.9 %collective-permute-start.20 = (bf16[8,112,384]{2,1,0:T(8,128)(2,1)S(1)}, bf16[8,112,384]{2,1,0:T(8,128)(2,1)}, u32[]{:S(2)}, u32[]{:S(2)}) collective-permute-start(bf16[8,112,384]{2,1,0:T(8,128)(2,1)S(1)} %pad_maximum_fusion.7.rest_0_), channel_id=1, source_target_pairs={{0,1},{1,0},{2,3},{3,2},{4,5},{5,4},{6,7},{7,6},{8,9},{9,8},{10,11... | collective-permute-start | bytes 2064392 | tf_op jit(solution)/shard_map/ppermute | solution.py:472
  64.3 33.9 %collective-permute-start.19 = (bf16[8,112,384]{2,1,0:T(8,128)(2,1)S(1)}, bf16[8,112,384]{2,1,0:T(8,128)(2,1)}, u32[]{:S(2)}, u32[]{:S(2)}) collective-permute-start(bf16[8,112,384]{2,1,0:T(8,128)(2,1)S(1)} %pad_maximum_fusion.7.rest_0_), channel_id=1, source_target_pairs={{0,4},{1,5},{2,6},{3,7},{4,0},{5,1},{6,2},{7,3},{8,12},{9,13},{10,... | collective-permute-start | bytes 2064392 | tf_op jit(solution)/shard_map/ppermute | solution.py:472
  78.5 26.5 %collective-permute-start.18 = (bf16[8,112,384]{2,1,0:T(8,128)(2,1)}, bf16[8,112,384]{2,1,0:T(8,128)(2,1)S(1)}, u32[]{:S(2)}, u32[]{:S(2)}) collective-permute-start(bf16[8,112,384]{2,1,0:T(8,128)(2,1)} %collective-permute-done.16.rest_5_), channel_id=1, source_target_pairs={{0,1},{1,0},{2,3},{3,2},{4,5},{5,4},{6,7},{7,6},{8,9},{9,8},{10,11... | collective-permute-start | bytes 2064392 | tf_op jit(solution)/shard_map/ppermute | solution.py:472
  98.2 9.3 %collective-permute-start.21 = (bf16[8,112,384]{2,1,0:T(8,128)(2,1)}, bf16[8,112,384]{2,1,0:T(8,128)(2,1)S(1)}, u32[]{:S(2)}, u32[]{:S(2)}) collective-permute-start(bf16[8,112,384]{2,1,0:T(8,128)(2,1)} %collective-permute-done.19.rest_1_), channel_id=1, source_target_pairs={{0,1},{1,0},{2,3},{3,2},{4,5},{5,4},{6,7},{7,6},{8,9},{9,8},{10,11... | collective-permute-start | bytes 2064392 | tf_op jit(solution)/shard_map/ppermute | solution.py:472
  105.0 2.5 copy-start.22
  143.5 12.2 %collective-permute-start.22 = (bf16[16,112,384]{2,1,0:T(8,128)(2,1)}, bf16[16,112,384]{2,1,0:T(8,128)(2,1)S(1)}, u32[]{:S(2)}, u32[]{:S(2)}) collective-permute-start(bf16[16,112,384]{2,1,0:T(8,128)(2,1)} %get-tuple-element.41), channel_id=1, source_target_pairs={{0,1},{1,0},{2,3},{3,2},{4,5},{5,4},{6,7},{7,6},{8,9},{9,8},{10,11... | collective-permute-start | bytes 4128776 | tf_op jit(solution)/shard_map/ppermute | solution.py:472
  151.6 1.0 copy-start.11
  152.6 3.1 copy-start.5
  152.7 4.4 %collective-permute-start.23 = (bf16[16,112,384]{2,1,0:T(8,128)(2,1)S(1)}, bf16[16,112,384]{2,1,0:T(8,128)(2,1)S(1)}, u32[]{:S(2)}, u32[]{:S(2)}) collective-permute-start(bf16[16,112,384]{2,1,0:T(8,128)(2,1)S(1)} %pad_maximum_fusion), channel_id=1, source_target_pairs={{0,1},{1,0},{2,3},{3,2},{4,5},{5,4},{6,7},{7,6},{8,9},{9,8},{10,11... | collective-permute-start | bytes 4128776 | tf_op jit(solution)/shard_map/ppermute | solution.py:472
  155.7 1.7 copy-start.13
  156.1 1.3 copy-start
  185.2 54.3 %copy-start.21 = (f32[1,3072]{1,0:T(1,128)S(1)}, f32[1,3072]{1,0:T(1,128)}, u32[]{:S(2)}) copy-start(f32[1,3072]{1,0:T(1,128)} %get-tuple-element.60) | copy-start | bytes 36868
  187.2 68.4 %collective-permute-start.33 = (bf16[8,112,384]{2,1,0:T(8,128)(2,1)}, bf16[8,112,384]{2,1,0:T(8,128)(2,1)}, u32[]{:S(2)}, u32[]{:S(2)}) collective-permute-start(bf16[8,112,384]{2,1,0:T(8,128)(2,1)} %slice.374), channel_id=1, source_target_pairs={{0,4},{1,5},{2,6},{3,7},{4,0},{5,1},{6,2},{7,3},{8,12},{9,13},{10,... | collective-permute-start | bytes 2064392 | tf_op jit(solution)/shard_map/ppermute | solution.py:472
  239.9 18.8 %collective-permute-start.35 = (bf16[8,112,384]{2,1,0:T(8,128)(2,1)}, bf16[8,112,384]{2,1,0:T(8,128)(2,1)S(1)}, u32[]{:S(2)}, u32[]{:S(2)}) collective-permute-start(bf16[8,112,384]{2,1,0:T(8,128)(2,1)} %slice.378), channel_id=1, source_target_pairs={{0,2},{1,3},{2,0},{3,1},{4,6},{5,7},{6,4},{7,5},{8,10},{9,11},{10,... | collective-permute-start | bytes 2064392 | tf_op jit(solution)/shard_map/ppermute | solution.py:472
  241.2 31.3 %collective-permute-start.24 = (bf16[16,112,384]{2,1,0:T(8,128)(2,1)}, bf16[16,112,384]{2,1,0:T(8,128)(2,1)S(1)}, u32[]{:S(2)}, u32[]{:S(2)}) collective-permute-start(bf16[16,112,384]{2,1,0:T(8,128)(2,1)} %get-tuple-element.58), channel_id=1, source_target_pairs={{0,1},{1,0},{2,3},{3,2},{4,5},{5,4},{6,7},{7,6},{8,9},{9,8},{10,11... | collective-permute-start | bytes 4128776 | tf_op jit(solution)/shard_map/ppermute | solution.py:472
  241.6 1.5 copy-start.15
  241.6 1.7 copy-start.3
  242.4 1.2 copy-start.17
  242.4 13.2 %copy-start.1 = (bf16[16,112,384]{2,1,0:T(8,128)(2,1)S(1)}, bf16[16,112,384]{2,1,0:T(8,128)(2,1)}, u32[]{:S(2)}) copy-start(bf16[16,112,384]{2,1,0:T(8,128)(2,1)} %copy-done) | copy-start | bytes 4128772
  242.6 30.9 %collective-permute-start.27 = (bf16[16,112,384]{2,1,0:T(8,128)(2,1)S(1)}, bf16[16,112,384]{2,1,0:T(8,128)(2,1)S(1)}, u32[]{:S(2)}, u32[]{:S(2)}) collective-permute-start(bf16[16,112,384]{2,1,0:T(8,128)(2,1)S(1)} %pad_maximum_fusion.1), channel_id=1, source_target_pairs={{0,1},{1,0},{2,3},{3,2},{4,5},{5,4},{6,7},{7,6},{8,9},{9,8},{10,11... | collective-permute-start | bytes 4128776 | tf_op jit(solution)/shard_map/ppermute | solution.py:472
  256.9 3.4 %copy-start.19 = (bf16[8,112,384]{2,1,0:T(8,128)(2,1)S(1)}, bf16[8,112,384]{2,1,0:T(8,128)(2,1)}, u32[]{:S(2)}) copy-start(bf16[8,112,384]{2,1,0:T(8,128)(2,1)} %copy-done.18) | copy-start | bytes 2064388
  256.9 10.0 %collective-permute-start.34 = (bf16[4,112,384]{2,1,0:T(8,128)(2,1)S(1)}, bf16[4,112,384]{2,1,0:T(8,128)(2,1)S(1)}, u32[]{:S(2)}, u32[]{:S(2)}) collective-permute-start(bf16[4,112,384]{2,1,0:T(8,128)(2,1)S(1)} %slice.376), channel_id=1, source_target_pairs={{0,2},{1,3},{2,0},{3,1},{4,6},{5,7},{6,4},{7,5},{8,10},{9,11},{10,... | collective-permute-start | bytes 1032200 | tf_op jit(solution)/shard_map/ppermute | solution.py:472
  258.9 9.8 %collective-permute-start.36 = (bf16[4,112,384]{2,1,0:T(8,128)(2,1)S(1)}, bf16[4,112,384]{2,1,0:T(8,128)(2,1)S(1)}, u32[]{:S(2)}, u32[]{:S(2)}) collective-permute-start(bf16[4,112,384]{2,1,0:T(8,128)(2,1)S(1)} %slice.380), channel_id=1, source_target_pairs={{0,4},{1,5},{2,6},{3,7},{4,0},{5,1},{6,2},{7,3},{8,12},{9,13},{10,... | collective-permute-start | bytes 1032200 | tf_op jit(solution)/shard_map/ppermute | solution.py:472
  260.3 12.2 %copy-start.4 = (bf16[16,112,384]{2,1,0:T(8,128)(2,1)S(1)}, bf16[16,112,384]{2,1,0:T(8,128)(2,1)}, u32[]{:S(2)}) copy-start(bf16[16,112,384]{2,1,0:T(8,128)(2,1)} %get-tuple-element.57) | copy-start | bytes 4128772
  268.9 7.9 %collective-permute-start.37 = (bf16[224,384]{1,0:T(8,128)(2,1)S(1)}, bf16[224,384]{1,0:T(8,128)(2,1)S(1)}, u32[]{:S(2)}, u32[]{:S(2)}) collective-permute-start(bf16[224,384]{1,0:T(8,128)(2,1)S(1)} %get-tuple-element.75), channel_id=1, source_target_pairs={{0,8},{1,9},{2,10},{3,11},{4,12},{5,13},{6,14},{7,15},{8,0},{9,1},... | collective-permute-start | bytes 516104 | tf_op jit(solution)/shard_map/ppermute | solution.py:472
  269.0 10.5 %collective-permute-start.39 = (bf16[224,384]{1,0:T(8,128)(2,1)S(1)}, bf16[224,384]{1,0:T(8,128)(2,1)S(1)}, u32[]{:S(2)}, u32[]{:S(2)}) collective-permute-start(bf16[224,384]{1,0:T(8,128)(2,1)S(1)} %get-tuple-element.76), channel_id=1, source_target_pairs={{0,24},{1,25},{2,26},{3,27},{4,28},{5,29},{6,30},{7,31},{8,16},{9,... | collective-permute-start | bytes 516104 | tf_op jit(solution)/shard_map/ppermute | solution.py:472
  270.7 15.7 %collective-permute-start.38 = (bf16[224,384]{1,0:T(8,128)(2,1)S(1)}, bf16[224,384]{1,0:T(8,128)(2,1)S(1)}, u32[]{:S(2)}, u32[]{:S(2)}) collective-permute-start(bf16[224,384]{1,0:T(8,128)(2,1)S(1)} %get-tuple-element.77), channel_id=1, source_target_pairs={{0,16},{1,17},{2,18},{3,19},{4,20},{5,21},{6,22},{7,23},{8,24},{9,... | collective-permute-start | bytes 516104 | tf_op jit(solution)/shard_map/ppermute | solution.py:472
  272.5 1.0 copy-start.12
  272.9 15.5 %collective-permute-start.25 = (bf16[8,112,384]{2,1,0:T(8,128)(2,1)S(1)}, bf16[8,112,384]{2,1,0:T(8,128)(2,1)S(1)}, u32[]{:S(2)}, u32[]{:S(2)}) collective-permute-start(bf16[8,112,384]{2,1,0:T(8,128)(2,1)S(1)} %slice.357), channel_id=1, source_target_pairs={{0,4},{1,5},{2,6},{3,7},{4,0},{5,1},{6,2},{7,3},{8,12},{9,13},{10,... | collective-permute-start | bytes 2064392 | tf_op jit(solution)/shard_map/ppermute | solution.py:472
  273.5 1.4 copy-start.23
  273.9 16.4 %collective-permute-start.28 = (bf16[8,112,384]{2,1,0:T(8,128)(2,1)S(1)}, bf16[8,112,384]{2,1,0:T(8,128)(2,1)S(1)}, u32[]{:S(2)}, u32[]{:S(2)}) collective-permute-start(bf16[8,112,384]{2,1,0:T(8,128)(2,1)S(1)} %slice.363), channel_id=1, source_target_pairs={{0,2},{1,3},{2,0},{3,1},{4,6},{5,7},{6,4},{7,5},{8,10},{9,11},{10,... | collective-permute-start | bytes 2064392 | tf_op jit(solution)/shard_map/ppermute | solution.py:472
  288.6 8.1 %collective-permute-start.26 = (bf16[4,112,384]{2,1,0:T(8,128)(2,1)S(1)}, bf16[4,112,384]{2,1,0:T(8,128)(2,1)S(1)}, u32[]{:S(2)}, u32[]{:S(2)}) collective-permute-start(bf16[4,112,384]{2,1,0:T(8,128)(2,1)S(1)} %slice.359), channel_id=1, source_target_pairs={{0,2},{1,3},{2,0},{3,1},{4,6},{5,7},{6,4},{7,5},{8,10},{9,11},{10,... | collective-permute-start | bytes 1032200 | tf_op jit(solution)/shard_map/ppermute | solution.py:472
  290.5 7.8 %collective-permute-start.29 = (bf16[4,112,384]{2,1,0:T(8,128)(2,1)S(1)}, bf16[4,112,384]{2,1,0:T(8,128)(2,1)S(1)}, u32[]{:S(2)}, u32[]{:S(2)}) collective-permute-start(bf16[4,112,384]{2,1,0:T(8,128)(2,1)S(1)} %slice.365), channel_id=1, source_target_pairs={{0,4},{1,5},{2,6},{3,7},{4,0},{5,1},{6,2},{7,3},{8,12},{9,13},{10,... | collective-permute-start | bytes 1032200 | tf_op jit(solution)/shard_map/ppermute | solution.py:472
  298.5 6.0 %collective-permute-start.30 = (bf16[224,384]{1,0:T(8,128)(2,1)S(1)}, bf16[224,384]{1,0:T(8,128)(2,1)S(1)}, u32[]{:S(2)}, u32[]{:S(2)}) collective-permute-start(bf16[224,384]{1,0:T(8,128)(2,1)S(1)} %get-tuple-element.72), channel_id=1, source_target_pairs={{0,8},{1,9},{2,10},{3,11},{4,12},{5,13},{6,14},{7,15},{8,0},{9,1},... | collective-permute-start | bytes 516104 | tf_op jit(solution)/shard_map/ppermute | solution.py:472
  299.5 7.8 %collective-permute-start.32 = (bf16[224,384]{1,0:T(8,128)(2,1)S(1)}, bf16[224,384]{1,0:T(8,128)(2,1)S(1)}, u32[]{:S(2)}, u32[]{:S(2)}) collective-permute-start(bf16[224,384]{1,0:T(8,128)(2,1)S(1)} %get-tuple-element.73), channel_id=1, source_target_pairs={{0,24},{1,25},{2,26},{3,27},{4,28},{5,29},{6,30},{7,31},{8,16},{9,... | collective-permute-start | bytes 516104 | tf_op jit(solution)/shard_map/ppermute | solution.py:472
  301.0 11.9 %collective-permute-start.31 = (bf16[224,384]{1,0:T(8,128)(2,1)S(1)}, bf16[224,384]{1,0:T(8,128)(2,1)S(1)}, u32[]{:S(2)}, u32[]{:S(2)}) collective-permute-start(bf16[224,384]{1,0:T(8,128)(2,1)S(1)} %get-tuple-element.74), channel_id=1, source_target_pairs={{0,16},{1,17},{2,18},{3,19},{4,20},{5,21},{6,22},{7,23},{8,24},{9,... | collective-permute-start | bytes 516104 | tf_op jit(solution)/shard_map/ppermute | solution.py:472
  (3 other events, 2.8 us)
